TPU v7x, 512 devices: a whole 4x4x16 slice. The times are simulated.
512 devices in a mesh: frame: 32 (over z_lo, x), freq: 16 (over z_hi, y, core).
Axes of the slice: x: 4, y: 4, z: 16 (z_hi: 2, z_lo: 8; z = z_hi * 8 + z_lo), core: 2. Of those that a mesh axis runs over, the one named last changes fastest.
Arguments:
- spectrum: float32 [8192, 16384], P('freq', 'frame'), may hold values from 0.1 to 10
- basis: float32 [8192, 128], P(('freq', 'frame')), may hold values from 0.02 to 0.5
- activations: float32 [16384, 128], P(('frame', 'freq')), may hold values from 0.02 to 0.5
Outputs:
- basis_out: float32 [8192, 128], P(('freq', 'frame'))
- activations_out: float32 [16384, 128], P(('frame', 'freq'))
All inputs are finite; a program needn't handle non-finite values.
Results may differ from a plain program's by a relative error of at most 0.0001.
Values sent between devices are 32-bit elements; how exact they have to be, the bound alone decides.
A program may use at most 64 MiB of HBM per device.

v0:
```python
import jax
import jax.numpy as jnp
from jax import lax
from jax.sharding import PartitionSpec as P

ITERS = 2


def product(left, right, contract_left, contract_right):
    return lax.dot_general(
        left,
        right,
        (((contract_left,), (contract_right,)), ((), ())),
        precision=lax.Precision.HIGHEST,
        preferred_element_type=jnp.float32,
    )


def gather_acts(owned):
    return lax.all_gather(owned, "freq", axis=0, tiled=True)


def gather_basis(owned):
    return lax.all_gather(owned, "frame", axis=0, tiled=True)


def per_device(spectrum, basis, activations):
    basis_owned = basis
    acts_owned = activations
    acts_panel = gather_acts(acts_owned)
    basis_panel = gather_basis(basis_owned)
    for sweep in range(ITERS):
        basis_total = lax.psum(jnp.sum(basis_panel, axis=0), "freq")
        quotient = spectrum / product(basis_panel, acts_panel, 1, 1)
        block = quotient
        numerator = lax.psum_scatter(
            product(block, basis_panel, 0, 0), "freq", scatter_dimension=0, tiled=True
        )
        acts_owned = acts_owned * numerator / basis_total[None, :]
        acts_panel = gather_acts(acts_owned)
        acts_total = lax.psum(jnp.sum(acts_panel, axis=0), "frame")
        quotient = spectrum / product(basis_panel, acts_panel, 1, 1)
        numerator = lax.psum_scatter(
            product(quotient, acts_panel, 1, 0), "frame", scatter_dimension=0, tiled=True
        )
        basis_owned = basis_owned * numerator / acts_total[None, :]
        if sweep + 1 < ITERS:
            basis_panel = gather_basis(basis_owned)
    return (basis_owned, acts_owned)


def solution(mesh):
    return jax.shard_map(
        per_device,
        mesh=mesh,
        in_specs=(P("freq", "frame"), P(("freq", "frame"), None), P(("frame", "freq"), None)),
        out_specs=(P(("freq", "frame"), None), P(("frame", "freq"), None)),
        check_vma=False,
    )
```

profile of v0, /device:TPU:6, one launch (start us, length us, event | category | flops | bytes accessed | tf_op | source)
XLA Modules:
  0.0 1031.9 jit_solution(114065835960727638)
XLA Ops:
  7.2 0.0 copy-start
  7.2 0.0 reduce-scatter.5.cloned.1.call-start
  7.2 109.3 %all_gather.15 = f32[512,128]{1,0:T(8,128)S(1)} all-gather(f32[16,128]{1,0:T(8,128)} %param.4), channel_id=1, replica_groups=mesh['frame'=32,'freq'=16] {'frame'}, dimensions={0}, use_global_device_ids=true | all-gather | bytes 270336 | tf_op jit(solution)/shard_map/all_gather | solution.py:24
  116.5 0.0 copy-done
  116.6 45.1 %all_gather.16 = f32[512,128]{1,0:T(8,128)S(1)} all-gather(f32[32,128]{1,0:T(8,128)S(1)} %copy-done), channel_id=1, replica_groups=mesh['frame'=32,'freq'=16] {'freq'}, dimensions={0}, use_global_device_ids=true | all-gather | bytes 278528 | tf_op jit(solution)/shard_map/all_gather | solution.py:20
  161.6 2.3 convolution_divide_fusion.2
  163.9 0.0 copy-start.3
  163.9 2.5 fusion.1
  166.4 0.0 reduce-scatter.5.cloned.1.call-update
  166.5 0.0 reduce-scatter.7.cloned.1.call-start
  166.5 0.1 reduce_sum.36
  166.6 62.3 %psum.28 = f32[128]{0:T(128)S(1)} all-reduce(f32[128]{0:T(128)S(1)} %reduce_sum.36), channel_id=1, replica_groups=mesh['frame'=32,'freq'=16] {'freq'}, use_global_device_ids=true, to_apply=%region_2.0 | all-reduce | flops 128 | bytes 1024 | tf_op jit(solution)/shard_map/psum | solution.py:33
  228.9 40.0 %reduce-scatter.5.cloned.1.call-done = f32[32,128]{1,0:T(8,128)} async-done(((f32[512,128]{1,0:T(8,128)}), f32[32,128]{1,0:T(8,128)}) %reduce-scatter.5.cloned.1.call-update) | async-done | bytes 16400 | tf_op jit(solution)/shard_map/reduce_scatter | solution.py:36
  268.9 0.7 multiply_divide_fusion.1
  269.6 36.7 %all_gather.17 = f32[512,128]{1,0:T(8,128)S(1)} all-gather(f32[32,128]{1,0:T(8,128)S(1)} %multiply_divide_fusion.1), channel_id=1, replica_groups=mesh['frame'=32,'freq'=16] {'freq'}, dimensions={0}, use_global_device_ids=true | all-gather | bytes 278528 | tf_op jit(solution)/shard_map/all_gather | solution.py:20
  306.3 0.0 copy-done.3
  306.3 1.0 fusion
  307.4 1.7 fusion.2
  309.0 0.0 reduce-scatter.7.cloned.1.call-update
  309.1 0.0 copy-start.2
  309.1 0.0 reduce-scatter.9.cloned.1.call-start
  309.1 0.1 reduce_sum.37
  309.2 104.0 %psum.29 = f32[128]{0:T(128)S(1)} all-reduce(f32[128]{0:T(128)S(1)} %reduce_sum.37), channel_id=1, replica_groups=mesh['frame'=32,'freq'=16] {'frame'}, use_global_device_ids=true, to_apply=%region_5.0 | all-reduce | flops 128 | bytes 1024 | tf_op jit(solution)/shard_map/psum | solution.py:41
  413.2 116.8 %reduce-scatter.7.cloned.1.call-done = f32[16,128]{1,0:T(8,128)} async-done(((f32[512,128]{1,0:T(8,128)}), f32[16,128]{1,0:T(8,128)}) %reduce-scatter.7.cloned.1.call-update) | async-done | bytes 8208 | tf_op jit(solution)/shard_map/reduce_scatter | solution.py:43
  530.0 0.0 copy-done.2
  530.0 0.7 multiply_divide_fusion.3
  530.7 122.4 %all_gather.18 = f32[512,128]{1,0:T(8,128)S(1)} all-gather(f32[16,128]{1,0:T(8,128)S(1)} %multiply_divide_fusion.3), channel_id=1, replica_groups=mesh['frame'=32,'freq'=16] {'frame'}, dimensions={0}, use_global_device_ids=true | all-gather | bytes 270336 | tf_op jit(solution)/shard_map/all_gather | solution.py:24
  653.1 1.0 convolution_divide_fusion.1
  654.1 2.5 fusion.3
  656.7 0.0 reduce-scatter.9.cloned.1.call-update
  656.7 0.0 reduce-scatter.11.cloned.1.call-start
  656.7 0.1 reduce_sum.38
  656.8 62.0 %psum.30 = f32[128]{0:T(128)S(1)} all-reduce(f32[128]{0:T(128)S(1)} %reduce_sum.38), channel_id=1, replica_groups=mesh['frame'=32,'freq'=16] {'freq'}, use_global_device_ids=true, to_apply=%region_8.0 | all-reduce | flops 128 | bytes 1024 | tf_op jit(solution)/shard_map/psum | solution.py:33
  718.8 43.7 %reduce-scatter.9.cloned.1.call-done = f32[32,128]{1,0:T(8,128)} async-done(((f32[512,128]{1,0:T(8,128)}), f32[32,128]{1,0:T(8,128)}) %reduce-scatter.9.cloned.1.call-update) | async-done | bytes 16400 | tf_op jit(solution)/shard_map/reduce_scatter | solution.py:36
  762.5 0.7 multiply_divide_fusion
  763.3 0.0 copy-start.1
  763.3 36.8 %all_gather.19 = f32[512,128]{1,0:T(8,128)S(1)} all-gather(f32[32,128]{1,0:T(8,128)S(1)} %multiply_divide_fusion), channel_id=1, replica_groups=mesh['frame'=32,'freq'=16] {'freq'}, dimensions={0}, use_global_device_ids=true | all-gather | bytes 278528 | tf_op jit(solution)/shard_map/all_gather | solution.py:20
  800.0 0.0 copy-done.1
  800.0 1.0 convolution_divide_fusion
  801.1 1.7 fusion.4
  802.8 0.0 reduce-scatter.11.cloned.1.call-update
  802.8 0.1 reduce_sum.39
  802.9 104.0 %psum.31 = f32[128]{0:T(128)S(1)} all-reduce(f32[128]{0:T(128)S(1)} %reduce_sum.39), channel_id=1, replica_groups=mesh['frame'=32,'freq'=16] {'frame'}, use_global_device_ids=true, to_apply=%region_11.0 | all-reduce | flops 128 | bytes 1024 | tf_op jit(solution)/shard_map/psum | solution.py:41
  906.9 117.2 %reduce-scatter.11.cloned.1.call-done = f32[16,128]{1,0:T(8,128)} async-done(((f32[512,128]{1,0:T(8,128)}), f32[16,128]{1,0:T(8,128)}) %reduce-scatter.11.cloned.1.call-update) | async-done | bytes 8208 | tf_op jit(solution)/shard_map/reduce_scatter | solution.py:43
  1024.1 1.3 multiply_divide_fusion.2
Async XLA Ops:
  7.2 109.4 %copy-start = (f32[32,128]{1,0:T(8,128)S(1)}, f32[32,128]{1,0:T(8,128)}, u32[]{:S(2)}) copy-start(f32[32,128]{1,0:T(8,128)} %param.5) | copy-start | bytes 49156
  7.2 261.7 %reduce-scatter.5.cloned.1.call-start = ((), (), s32[]{:S(2)}) async-start(), calls=%async_computation.4 | async-start | bytes 278528 | tf_op jit(solution)/shard_map/reduce_scatter | solution.py:36
  163.9 142.4 %copy-start.3 = (f32[512,512]{1,0:T(8,128)S(1)}, f32[512,512]{1,0:T(8,128)}, u32[]{:S(2)}) copy-start(f32[512,512]{1,0:T(8,128)} %param.3) | copy-start | bytes 3145732
  166.5 363.6 %reduce-scatter.7.cloned.1.call-start = ((), (), s32[]{:S(2)}) async-start(), calls=%async_computation.5 | async-start | bytes 270336 | tf_op jit(solution)/shard_map/reduce_scatter | solution.py:43
  309.1 221.0 %copy-start.2 = (f32[16,128]{1,0:T(8,128)S(1)}, f32[16,128]{1,0:T(8,128)}, u32[]{:S(2)}) copy-start(f32[16,128]{1,0:T(8,128)} %param.4) | copy-start | bytes 24580
  309.1 453.5 %reduce-scatter.9.cloned.1.call-start = ((), (), s32[]{:S(2)}) async-start(), calls=%async_computation.6 | async-start | bytes 278528 | tf_op jit(solution)/shard_map/reduce_scatter | solution.py:36
  656.7 367.4 %reduce-scatter.11.cloned.1.call-start = ((), (), s32[]{:S(2)}) async-start(), calls=%async_computation.7 | async-start | bytes 270336 | tf_op jit(solution)/shard_map/reduce_scatter | solution.py:43
  763.3 36.8 %copy-start.1 = (f32[32,128]{1,0:T(8,128)}, f32[32,128]{1,0:T(8,128)S(1)}, u32[]{:S(2)}) copy-start(f32[32,128]{1,0:T(8,128)S(1)} %multiply_divide_fusion) | copy-start | bytes 49156
Sparse Core Ops, SparseCore 0:
  166.6 102.2 reduce-scatter.4
  309.2 220.8 reduce-scatter.6
  656.8 105.6 reduce-scatter.8
  802.9 221.0 reduce-scatter.10
where the time goes:
time: 1050 us; the launch traced here: 1030 us
  blocking collectives  683 us (65%)
  waiting for transfers between devices  318 us (30%)
  matrix products  13.8 us (1%)
  between operations  13.8 us (1%)
    reduce_scatter x2, waiting for transfers between devices, per_device(): lax.psum_scatter(product(quotient, acts_panel, 1, 0), 'frame', scatter_di...  234 us
    all_gather x2, blocking collectives, gather_basis(): return lax.all_gather(owned, 'frame', axis=0, tiled=True)  232 us
    psum x2, blocking collectives, per_device(): acts_total = lax.psum(jnp.sum(acts_panel, axis=0), 'frame')  208 us
    psum x2, blocking collectives, per_device(): basis_total = lax.psum(jnp.sum(basis_panel, axis=0), 'freq')  124 us
    all_gather x3, blocking collectives, gather_acts(): return lax.all_gather(owned, 'freq', axis=0, tiled=True)  119 us
    reduce_scatter x2, waiting for transfers between devices, per_device(): lax.psum_scatter(product(block, basis_panel, 0, 0), 'freq', scatter_dimen...  83.7 us
  transfers between devices with their start and end apart: 4, of which 4 were waited for; matrix products, arithmetic and copies ran while one was open for 0% of the time, Pallas kernels for 0%

commit v1 on v0

v1 whole, which is shorter than its diff:
```python
import jax
import jax.numpy as jnp
from jax import lax
from jax.experimental import pallas as pl
from jax.experimental.pallas import tpu as pltpu
from jax.sharding import PartitionSpec as P

ITERS = 2
K = 128
X, ZR, ZQ = 4, 4, 2
Y, ZH, C = 4, 2, 2
F32, BF16 = jnp.float32, jnp.bfloat16


def halves(value):
    high = value.astype(BF16)
    return high, (value - high.astype(F32)).astype(BF16)


def dot3(left, right, contract_right):
    dims = (((1,), (contract_right,)), ((), ()))

    def one(a, b):
        return lax.dot_general(a, b, dims, preferred_element_type=F32)

    return one(left[0], right[0]) + (one(left[0], right[1]) + one(left[1], right[0]))


def fold8(value):
    return jnp.sum(value.reshape(value.shape[0] // 8, 8, K), axis=0)


def kernel(
    spec_hbm, basis_ref, acts_ref, basis_out, acts_out,
    spec, spec_t, wp, gp,
    fcore, fcore_in, fy, fy_in, fz, fz_in,
    rx, rx_in, rr, rr_in, rq, rq_in,
    spec_sem, send_sem, recv_sem,
):
    fr = lax.axis_index("frame")
    fq = lax.axis_index("freq")
    x, zl = lax.rem(fr, X), lax.div(fr, X)
    zr, zq = lax.rem(zl, ZR), lax.div(zl, ZR)
    c, yz = lax.rem(fq, C), lax.div(fq, C)
    y, zh = lax.rem(yz, Y), lax.div(yz, Y)
    bins, frames = spec.shape
    wrows, grows = basis_ref.shape[0], acts_ref.shape[0]

    def frame_at(zq_, zr_, x_):
        return ((zq_ * ZR + zr_) * X + x_, fq)

    def freq_at(zh_, y_, c_):
        return (fr, (zh_ * Y + y_) * C + c_)

    def step(value, by, size):
        return lax.rem(value + by, size)

    core_peer = freq_at(zh, y, 1 - c)
    y_peer = {d: freq_at(zh, step(y, d, Y), c) for d in range(1, Y)}
    zh_peer = freq_at(1 - zh, y, c)
    x_peer = {d: frame_at(zq, zr, step(x, d, X)) for d in range(1, X)}
    zr_peer = {d: frame_at(zq, step(zr, d, ZR), x) for d in range(1, ZR)}
    zq_peer = frame_at(1 - zq, zr, x)
    peers = [core_peer, zh_peer, zq_peer, *y_peer.values(), *x_peer.values(), *zr_peer.values()]

    spec_copy = pltpu.make_async_copy(spec_hbm, spec, spec_sem)
    spec_copy.start()

    barrier = pltpu.get_barrier_semaphore()
    for peer in peers:
        pl.semaphore_signal(barrier, inc=1, device_id=peer, device_id_type=pl.DeviceIdType.MESH)

    spec_copy.wait()
    for i in range(frames // 128):
        spec_t[pl.ds(128 * i, 128), :] = spec[:, pl.ds(128 * i, 128)].T

    pl.semaphore_wait(barrier, len(peers))

    copies = []

    def send(src, dst, peer):
        slot = len(copies)
        copy = pltpu.make_async_remote_copy(
            src_ref=src, dst_ref=dst, send_sem=send_sem.at[slot], recv_sem=recv_sem.at[slot],
            device_id=peer, device_id_type=pl.DeviceIdType.MESH,
        )
        copy.start()
        copies.append(copy)
        return copy

    def gather_acts(g):
        mine = g.at[:, y, c]
        near = {d: send(mine, mine, y_peer[d]) for d in (2, 1, 3)}
        waits = [send(mine, mine, core_peer)]
        for d in (1, 3, 2):
            near[d].wait_recv()
            there = g.at[:, step(y, Y - d, Y), c]
            waits.append(send(there, there, core_peer))
        for w in waits:
            w.wait_recv()

    def gather_basis(w):
        mine = w.at[:, zr, x]
        near = {d: send(mine, mine, zr_peer[d]) for d in range(1, ZR)}
        waits = [send(mine, mine, x_peer[d]) for d in (2, 1, 3)]
        for d in range(1, ZR):
            near[d].wait_recv()
            there = w.at[:, step(zr, ZR - d, ZR), x]
            for e in (2, 1, 3):
                waits.append(send(there, there, x_peer[e]))
        for wait in waits:
            wait.wait_recv()

    def reduce_freq(it):
        width = ZH * grows
        first = send(fcore.at[it, 1 - c], fcore_in.at[it], core_peer)
        first.wait_recv()
        total = fcore[it, c] + fcore_in[it]
        for i in range(Y):
            fy[it, i, pl.ds(0, width)] = total[i * width:(i + 1) * width]
            fy[it, i, pl.ds(width, 8)] = total[Y * width:]
        near = {d: send(fy.at[it, step(y, d, Y)], fy_in.at[it, d - 1], y_peer[d]) for d in (2, 1, 3)}
        total = fy[it, y]
        for d in (1, 3, 2):
            near[d].wait_recv()
            total = total + fy_in[it, d - 1]
        fz[it] = total
        far = send(fz.at[it], fz_in.at[it], zh_peer)
        far.wait_recv()
        total = total + fz_in[it]
        return total[:width].reshape(ZH, grows, K), jnp.sum(total[width:], axis=0)

    def reduce_frame(it):
        width = ZQ * wrows
        near = {d: send(rx.at[it, step(x, d, X)], rx_in.at[it, d - 1], x_peer[d]) for d in (2, 1, 3)}
        total = rx[it, x]
        for d in (1, 3, 2):
            near[d].wait_recv()
            total = total + rx_in[it, d - 1]
        for i in range(ZR):
            rr[it, i, pl.ds(0, width)] = total[i * width:(i + 1) * width]
            rr[it, i, pl.ds(width, 8)] = total[ZR * width:]
        near = {d: send(rr.at[it, step(zr, d, ZR)], rr_in.at[it, d - 1], zr_peer[d]) for d in (2, 1, 3)}
        total = rr[it, zr]
        for d in (1, 3, 2):
            near[d].wait_recv()
            total = total + rr_in[it, d - 1]
        rq[it] = total
        far = send(rq.at[it], rq_in.at[it], zq_peer)
        far.wait_recv()
        total = total + rq_in[it]
        return total[:width].reshape(ZQ, wrows, K), jnp.sum(total[width:], axis=0)

    far_acts = send(acts_ref, gp.at[0, zh, y, c], zh_peer)
    far_basis = send(basis_ref, wp.at[0, zq, zr, x], zq_peer)
    gp[0, zh, y, c] = acts_ref[...]
    wp[0, zq, zr, x] = basis_ref[...]
    far_basis.wait_recv()
    gather_basis(wp.at[0])
    far_acts.wait_recv()
    gather_acts(gp.at[0])

    rows = 128
    for it in range(ITERS):
        w_now = wp[it].reshape(bins, K)
        g_now = gp[it].reshape(frames, K)
        wh = halves(w_now)
        gh = halves(g_now)
        sums = fold8(w_now)
        for j in range(C):
            fcore[it, j, pl.ds(Y * ZH * grows, 8)] = sums
        for i in range(frames // rows):
            at = slice(i * rows, (i + 1) * rows)
            product = dot3((gh[0][at], gh[1][at]), wh, 1)
            quotient = spec_t[pl.ds(i * rows, rows), :] / product
            terms = dot3(halves(quotient), wh, 0)
            for b in range(rows // grows):
                q = i * (rows // grows) + b
                cc, yy, zz = q % C, (q // C) % Y, q // (C * Y)
                fcore[it, cc, pl.ds((yy * ZH + zz) * grows, grows)] = terms[b * grows:(b + 1) * grows]
        numerator, total = reduce_freq(it)
        fresh = gp[it, :, y, c] * numerator / total
        gp[it + 1, :, y, c] = fresh
        gather_acts(gp.at[it + 1])
        if it + 1 == ITERS:
            acts_out[...] = gp[it + 1, zh, y, c]

        g_now = gp[it + 1].reshape(frames, K)
        gh = halves(g_now)
        sums = fold8(g_now)
        for j in range(X):
            rx[it, j, pl.ds(ZR * ZQ * wrows, 8)] = sums
        for i in range(bins // rows):
            at = slice(i * rows, (i + 1) * rows)
            product = dot3((wh[0][at], wh[1][at]), gh, 1)
            quotient = spec[pl.ds(i * rows, rows), :] / product
            terms = dot3(halves(quotient), gh, 0)
            for b in range(rows // wrows):
                q = i * (rows // wrows) + b
                xx, rr_, qq = q % X, (q // X) % ZR, q // (X * ZR)
                rx[it, xx, pl.ds((rr_ * ZQ + qq) * wrows, wrows)] = terms[b * wrows:(b + 1) * wrows]
        numerator, total = reduce_frame(it)
        fresh = wp[it, :, zr, x] * numerator / total
        wp[it + 1, :, zr, x] = fresh
        if it + 1 < ITERS:
            gather_basis(wp.at[it + 1])
        else:
            basis_out[...] = wp[it + 1, zq, zr, x]

    for copy in copies:
        copy.wait_send()


def per_device(spectrum, basis, activations):
    bins, frames = spectrum.shape
    wrows, grows = basis.shape[0], activations.shape[0]
    fwide, rwide = Y * ZH * grows + 8, ZR * ZQ * wrows + 8
    fpart, rpart = ZH * grows + 8, ZQ * wrows + 8
    vmem = pl.BlockSpec(memory_space=pltpu.VMEM)
    return pl.pallas_call(
        kernel,
        out_shape=(
            jax.ShapeDtypeStruct(basis.shape, F32),
            jax.ShapeDtypeStruct(activations.shape, F32),
        ),
        in_specs=[pl.BlockSpec(memory_space=pl.ANY), vmem, vmem],
        out_specs=(vmem, vmem),
        scratch_shapes=[
            pltpu.VMEM((bins, frames), F32),
            pltpu.VMEM((frames, bins), F32),
            pltpu.VMEM((ITERS + 1, ZQ, ZR, X, wrows, K), F32),
            pltpu.VMEM((ITERS + 1, ZH, Y, C, grows, K), F32),
            pltpu.VMEM((ITERS, C, fwide, K), F32),
            pltpu.VMEM((ITERS, fwide, K), F32),
            pltpu.VMEM((ITERS, Y, fpart, K), F32),
            pltpu.VMEM((ITERS, Y - 1, fpart, K), F32),
            pltpu.VMEM((ITERS, fpart, K), F32),
            pltpu.VMEM((ITERS, fpart, K), F32),
            pltpu.VMEM((ITERS, X, rwide, K), F32),
            pltpu.VMEM((ITERS, X - 1, rwide, K), F32),
            pltpu.VMEM((ITERS, ZR, rpart, K), F32),
            pltpu.VMEM((ITERS, ZR - 1, rpart, K), F32),
            pltpu.VMEM((ITERS, rpart, K), F32),
            pltpu.VMEM((ITERS, rpart, K), F32),
            pltpu.SemaphoreType.DMA(()),
            pltpu.SemaphoreType.DMA((96,)),
            pltpu.SemaphoreType.DMA((96,)),
        ],
        compiler_params=pltpu.CompilerParams(
            collective_id=0, has_side_effects=True, vmem_limit_bytes=48 * 1024 * 1024
        ),
    )(spectrum, basis, activations)


def solution(mesh):
    return jax.shard_map(
        per_device,
        mesh=mesh,
        in_specs=(P("freq", "frame"), P(("freq", "frame"), None), P(("frame", "freq"), None)),
        out_specs=(P(("freq", "frame"), None), P(("frame", "freq"), None)),
        check_vma=False,
    )
```

time: 1050 us -> 116 us (0.11); the launches traced: 1030 us -> 114 us
  blocking collectives: 683 us -> 0 us
  waiting for transfers between devices: 318 us -> 0 us
  Pallas kernels: 0 us -> 110 us
  matrix products: 13.8 us -> 0 us
  between operations: 13.8 us -> 0.65 us
    all_gather x5 -> x0, blocking collectives: 350 us -> none  [the longest x2 232 us: gather_basis(): return lax.all_gather(owned, 'frame', axis=0, tiled=True)]
    psum x4 -> x0, blocking collectives: 332 us -> none  [the longest x2 208 us: per_device(): acts_total = lax.psum(jnp.sum(acts_panel, axis=0), 'frame')]
    reduce_scatter x4 -> x0, waiting for transfers between devices: 318 us -> none  [the longest x2 234 us: per_device(): lax.psum_scatter(product(quotient, acts_panel, 1, 0), 'frame', scatter_di...]
    pallas_call x0 -> x1, Pallas kernels: none -> 110 us  [per_device(): pl.pallas_call(kernel, out_shape=(jax.ShapeDtypeStruct(basis.shape, F32),...]
    dot_general x8 -> x0, matrix products: 13.8 us -> none  [product(): lax.dot_general(left, right, (((contract_left,), (contract_right,)), ((),...]
  transfers between devices with their start and end apart: 4 -> 0, of which waited for: 4 -> 0; matrix products, arithmetic and copies ran while one was open for 0% -> 0% of each run, Pallas kernels for 0% -> 0%
where the time goes in v1:
time: 116 us; the launch traced here: 114 us
  Pallas kernels  110 us (95%)
  local copies, waits for them, and re-layouts  3.84 us (3%)
    pallas_call x1, Pallas kernels, per_device(): pl.pallas_call(kernel, out_shape=(jax.ShapeDtypeStruct(basis.shape, F32),...  110 us
    unnamed x8, local copies, waits for them, and re-layouts  3.84 us

profile of v1, /device:TPU:6, one launch (start us, length us, event | category | flops | bytes accessed | tf_op | source)
XLA Modules:
  0.0 114.4 jit_solution(378667347043635704)
XLA Ops:
  0.6 0.0 copy-start
  0.6 1.2 %copy-done = f32[512,512]{1,0:T(8,128)S(1)} copy-done((f32[512,512]{1,0:T(8,128)S(1)}, f32[512,512]{1,0:T(8,128)}, u32[]{:S(2)}) %copy-start) | copy-done | bytes 1048600
  1.9 0.0 copy-start.1
  1.9 0.7 copy-done.1
  2.6 0.0 copy-start.2
  2.6 0.7 copy-done.2
  3.3 109.9 %shard_map.50 = (f32[16,128]{1,0:T(8,128)S(1)}, f32[32,128]{1,0:T(8,128)S(1)}) custom-call(f32[512,512]{1,0:T(8,128)S(1)} %copy-done, f32[16,128]{1,0:T(8,128)S(1)} %copy-done.2, f32[32,128]{1,0:T(8,128)S(1)} %copy-done.1), custom_call_target="tpu_custom_call" | custom-call | tf_op jit(solution)/shard_map/pallas_call | solution.py:220
  113.2 0.6 copy.7
  113.8 0.6 copy.8
Async XLA Ops:
  0.6 1.2 %copy-start = (f32[512,512]{1,0:T(8,128)S(1)}, f32[512,512]{1,0:T(8,128)}, u32[]{:S(2)}) copy-start(f32[512,512]{1,0:T(8,128)} %spec_hbm.1) | copy-start | bytes 3145732
  1.9 0.7 copy-start.1
  2.6 0.7 copy-start.2

commit v2 on v0

v2 whole, which is shorter than its diff:
```python
import jax
import jax.numpy as jnp
from jax import lax
from jax.experimental import pallas as pl
from jax.experimental.pallas import tpu as pltpu
from jax.sharding import PartitionSpec as P

ITERS = 2
K = 128
X, ZR, ZQ = 4, 4, 2
Y, ZH, C = 4, 2, 2
SEMS = 160
F32, BF16 = jnp.float32, jnp.bfloat16


def halves(value):
    high = value.astype(BF16)
    return high, (value - high.astype(F32)).astype(BF16)


def dot(left, right, contract_right):
    return lax.dot_general(
        left, right, (((1,), (contract_right,)), ((), ())), preferred_element_type=F32
    )


def outer(left, right):
    wide = dot(jnp.concatenate(left, axis=1), jnp.concatenate([right[0], right[0]], axis=1), 1)
    return wide + dot(left[0], right[1], 1)


def inner(left, right):
    wide = dot(left[0], jnp.concatenate(right, axis=1), 0)
    return wide[:, :K] + wide[:, K:] + dot(left[1], right[0], 0)


def fold8(value):
    return jnp.sum(value.reshape(-1, 8, K), axis=0)


def kernel(
    spec_hbm, basis_hbm, acts_hbm, basis_out, acts_out,
    raw, spec, spec_t, wp, gp,
    fcore, fcore_in, fy, fy_in, fz, fz_in,
    wacc, rx, rx_in, rs, rs_in, rq, rq_in,
    load_sem, send_sem, recv_sem,
):
    fr = lax.axis_index("frame")
    fq = lax.axis_index("freq")
    x, zl = lax.rem(fr, X), lax.div(fr, X)
    zr, zq = lax.rem(zl, ZR), lax.div(zl, ZR)
    c, yz = lax.rem(fq, C), lax.div(fq, C)
    y, zh = lax.rem(yz, Y), lax.div(yz, Y)
    wrows, grows = basis_hbm.shape[0], acts_hbm.shape[0]
    xbins, cframes = ZQ * ZR * wrows, ZH * Y * grows
    gpart, wpart = ZH * grows, ZQ * wrows

    def frame_at(zq_, zr_, x_):
        return ((zq_ * ZR + zr_) * X + x_, fq)

    def freq_at(zh_, y_, c_):
        return (fr, (zh_ * Y + y_) * C + c_)

    def step(value, by, size):
        return lax.rem(value + by, size)

    core_peer = freq_at(zh, y, 1 - c)
    zh_peer = freq_at(1 - zh, y, c)
    zq_peer = frame_at(1 - zq, zr, x)
    y_peer = {d: freq_at(zh, step(y, d, Y), c) for d in (2, 1, 3)}
    steps = [(d, e) for d in (2, 1, 3, 0) for e in (2, 1, 3, 0) if d or e]
    xz_peer = {(d, e): frame_at(zq, step(zr, e, ZR), step(x, d, X)) for d, e in steps}
    peers = [core_peer, zh_peer, zq_peer, *y_peer.values(), *xz_peer.values()]

    loads = [
        pltpu.make_async_copy(basis_hbm, wp.at[0, x, zq, zr], load_sem.at[0]),
        pltpu.make_async_copy(acts_hbm, gp.at[0, c, zh, y], load_sem.at[1]),
    ]
    for i in range(X):
        loads.append(pltpu.make_async_copy(spec_hbm.at[:, i], raw.at[i], load_sem.at[2 + i]))
    for load in loads:
        load.start()

    barrier = pltpu.get_barrier_semaphore()
    for peer in peers:
        pl.semaphore_signal(barrier, inc=1, device_id=peer, device_id_type=pl.DeviceIdType.MESH)

    for load in loads:
        load.wait()
    for i in range(X):
        turned = raw[i].reshape(xbins, C * cframes).T
        for j in range(C * ZH * Y):
            spec_t[i, j % C, pl.ds(j // C * grows, grows)] = turned[j * grows:(j + 1) * grows]
    for i in range(X):
        for j in range(C):
            spec[j, i] = spec_t[i, j].T

    pl.semaphore_wait(barrier, len(peers))

    copies = []

    def send(src, dst, peer):
        slot = len(copies)
        copy = pltpu.make_async_remote_copy(
            src_ref=src, dst_ref=dst, send_sem=send_sem.at[slot], recv_sem=recv_sem.at[slot],
            device_id=peer, device_id_type=pl.DeviceIdType.MESH,
        )
        copy.start()
        copies.append(copy)
        return copy

    def send_near(ref):
        return {d: send(ref, ref, y_peer[d]) for d in (2, 1, 3)}

    def send_plane(ref):
        return {at: send(ref, ref, xz_peer[at]) for at in steps}

    def wait_all(waits):
        for wait in waits:
            wait.wait_recv()

    def wait_near(near, part):
        passed = []
        for d in (1, 3, 2):
            near[d].wait_recv()
            there = part(step(y, Y - d, Y))
            passed.append(send(there, there, core_peer))
        return passed

    mine_w, mine_g = wp.at[0, x, zq, zr], gp.at[0, c, zh, y]
    far_g = send(mine_g, mine_g, zh_peer)
    far_w = send(mine_w, mine_w, zq_peer)
    near = send_near(mine_g)
    cross = [send(mine_g, mine_g, core_peer)]
    plane = send_plane(mine_w)
    cross += wait_near(near, lambda y_: gp.at[0, c, zh, y_])
    far_w.wait_recv()
    there = wp.at[0, x, 1 - zq, zr]
    plane_far = send_plane(there)
    far_g.wait_recv()
    there = gp.at[0, c, 1 - zh, y]
    near = send_near(there)
    cross.append(send(there, there, core_peer))
    wait_all(plane.values())
    wait_all(plane_far.values())
    cross += wait_near(near, lambda y_: gp.at[0, c, 1 - zh, y_])
    wait_all(cross)
    plane = None

    def acts_terms(it, c_, zh_, xs):
        w = halves(jnp.concatenate([wp[it, i].reshape(xbins, K) for i in xs], axis=0))
        g = halves(gp[it, c_, zh_].reshape(Y * grows, K))
        rows = pl.ds(zh_ * Y * grows, Y * grows)
        s = jnp.concatenate([spec_t[i, c_, rows] for i in xs], axis=1)
        return inner(halves(s / outer(g, w)), w)

    def basis_terms(it, x_, c_):
        w = halves(wp[it, x_].reshape(xbins, K))
        g = halves(gp[it + 1, c_].reshape(cframes, K))
        return inner(halves(spec[c_, x_] / outer(w, g)), g)

    for it in range(ITERS):
        if plane is not None:
            wait_all(plane[0, e] for e in range(1, ZR))
        for c_ in range(C):
            for zh_ in range(ZH):
                rows = pl.ds(zh_ * Y * grows, Y * grows)
                fcore[it, c_, rows] = acts_terms(it, c_, zh_, [x])
        if plane is not None:
            wait_all(plane[at] for at in steps if at[0])
        sums = fold8(wp[it])
        for c_ in range(C):
            fcore[it, c_, pl.ds(cframes, 8)] = sums
        others = [step(x, d, X) for d in (1, 3, 2)]
        for c_ in (1 - c, c):
            for zh_ in range(ZH):
                rows = pl.ds(zh_ * Y * grows, Y * grows)
                fcore[it, c_, rows] += acts_terms(it, c_, zh_, others)
            if c_ is not c:
                first = send(fcore.at[it, c_], fcore_in.at[it], core_peer)
        first.wait_recv()
        total = fcore[it, c] + fcore_in[it]
        for i in range(Y):
            for j in range(ZH):
                at = (j * Y + i) * grows
                fy[it, i, pl.ds(j * grows, grows)] = total[at:at + grows]
            fy[it, i, pl.ds(gpart, 8)] = total[cframes:]
        near = {d: send(fy.at[it, step(y, d, Y)], fy_in.at[it, d - 1], y_peer[d]) for d in (2, 1, 3)}
        total = fy[it, y]
        for d in (1, 3, 2):
            near[d].wait_recv()
            total = total + fy_in[it, d - 1]
        fz[it] = total
        far = send(fz.at[it], fz_in.at[it], zh_peer)
        far.wait_recv()
        total = total + fz_in[it]
        scale = jnp.sum(total[gpart:], axis=0)
        gp[it + 1, c, :, y] = gp[it, c, :, y] * total[:gpart].reshape(ZH, grows, K) / scale
        mine = gp.at[it + 1, c, :, y]
        near = send_near(mine)
        cross = [send(mine, mine, core_peer)]
        if it + 1 == ITERS:
            acts_out[...] = gp[it + 1, c, zh, y]
        cross += wait_near(near, lambda y_: gp.at[it + 1, c, :, y_])

        for i in range(X):
            wacc[i] = basis_terms(it, i, c)
        sums = fold8(gp[it + 1, c])
        wait_all(cross)
        sums = sums + fold8(gp[it + 1, 1 - c])
        rs[it] = sums
        totals = {at: send(rs.at[it], rs_in.at[it, at[0], at[1]], xz_peer[at]) for at in steps}
        plane = {}
        for d in (2, 1, 3, 0):
            x_ = step(x, d, X)
            terms = wacc[x_] + basis_terms(it, x_, 1 - c)
            for i in range(ZR):
                for j in range(ZQ):
                    at = (j * ZR + i) * wrows
                    rx[it, x_, i, pl.ds(j * wrows, wrows)] = terms[at:at + wrows]
            for at in steps:
                if at[0] == d:
                    src = rx.at[it, x_, step(zr, at[1], ZR)]
                    plane[at] = send(src, rx_in.at[it, at[0], at[1]], xz_peer[at])
        for at in steps:
            totals[at].wait_recv()
            sums = sums + rs_in[it, at[0], at[1]]
        total = rx[it, x, zr]
        for at in sorted(steps):
            plane[at].wait_recv()
            total = total + rx_in[it, at[0], at[1]]
        rq[it, pl.ds(0, wpart)] = total
        rq[it, pl.ds(wpart, 8)] = sums
        far = send(rq.at[it], rq_in.at[it], zq_peer)
        far.wait_recv()
        total = (total + rq_in[it, pl.ds(0, wpart)]).reshape(ZQ, wrows, K)
        scale = jnp.sum(sums + rq_in[it, pl.ds(wpart, 8)], axis=0)
        wp[it + 1, x, :, zr] = wp[it, x, :, zr] * total / scale
        if it + 1 < ITERS:
            plane = send_plane(wp.at[it + 1, x, :, zr])
        else:
            basis_out[...] = wp[it + 1, x, zq, zr]

    for copy in copies:
        copy.wait_send()


def per_device(spectrum, basis, activations):
    bins, frames = spectrum.shape
    wrows, grows = basis.shape[0], activations.shape[0]
    gpart, wpart = ZH * grows, ZQ * wrows
    fwide = Y * gpart + 8
    anywhere = pl.BlockSpec(memory_space=pl.ANY)
    vmem = pl.BlockSpec(memory_space=pltpu.VMEM)
    return pl.pallas_call(
        kernel,
        out_shape=(
            jax.ShapeDtypeStruct(basis.shape, F32),
            jax.ShapeDtypeStruct(activations.shape, F32),
        ),
        in_specs=[anywhere] * 3,
        out_specs=(vmem, vmem),
        scratch_shapes=[
            pltpu.VMEM((X, ZQ * ZR, wrows, frames), F32),
            pltpu.VMEM((C, X, bins // X, frames // C), F32),
            pltpu.VMEM((X, C, frames // C, bins // X), F32),
            pltpu.VMEM((ITERS + 1, X, ZQ, ZR, wrows, K), F32),
            pltpu.VMEM((ITERS + 1, C, ZH, Y, grows, K), F32),
            pltpu.VMEM((ITERS, C, fwide, K), F32),
            pltpu.VMEM((ITERS, fwide, K), F32),
            pltpu.VMEM((ITERS, Y, gpart + 8, K), F32),
            pltpu.VMEM((ITERS, Y - 1, gpart + 8, K), F32),
            pltpu.VMEM((ITERS, gpart + 8, K), F32),
            pltpu.VMEM((ITERS, gpart + 8, K), F32),
            pltpu.VMEM((X, bins // X, K), F32),
            pltpu.VMEM((ITERS, X, ZR, wpart, K), F32),
            pltpu.VMEM((ITERS, X, ZR, wpart, K), F32),
            pltpu.VMEM((ITERS, 8, K), F32),
            pltpu.VMEM((ITERS, X, ZR, 8, K), F32),
            pltpu.VMEM((ITERS, wpart + 8, K), F32),
            pltpu.VMEM((ITERS, wpart + 8, K), F32),
            pltpu.SemaphoreType.DMA((2 + X,)),
            pltpu.SemaphoreType.DMA((SEMS,)),
            pltpu.SemaphoreType.DMA((SEMS,)),
        ],
        compiler_params=pltpu.CompilerParams(
            collective_id=0, has_side_effects=True, vmem_limit_bytes=67_043_328
        ),
    )(spectrum.reshape(ZQ * ZR, X, wrows, frames), basis, activations)


def solution(mesh):
    return jax.shard_map(
        per_device,
        mesh=mesh,
        in_specs=(P("freq", "frame"), P(("freq", "frame"), None), P(("frame", "freq"), None)),
        out_specs=(P(("freq", "frame"), None), P(("frame", "freq"), None)),
        check_vma=False,
    )
```

time: 1050 us -> 108 us (0.10); the launches traced: 1030 us -> 107 us
  blocking collectives: 683 us -> 0 us
  waiting for transfers between devices: 318 us -> 0 us
  Pallas kernels: 0 us -> 104 us
  matrix products: 13.8 us -> 0 us
  between operations: 13.8 us -> 0.65 us
    all_gather x5 -> x0, blocking collectives: 350 us -> none  [the longest x2 232 us: gather_basis(): return lax.all_gather(owned, 'frame', axis=0, tiled=True)]
    psum x4 -> x0, blocking collectives: 332 us -> none  [the longest x2 208 us: per_device(): acts_total = lax.psum(jnp.sum(acts_panel, axis=0), 'frame')]
    reduce_scatter x4 -> x0, waiting for transfers between devices: 318 us -> none  [the longest x2 234 us: per_device(): lax.psum_scatter(product(quotient, acts_panel, 1, 0), 'frame', scatter_di...]
    pallas_call x0 -> x1, Pallas kernels: none -> 104 us  [per_device(): pl.pallas_call(kernel, out_shape=(jax.ShapeDtypeStruct(basis.shape, F32),...]
    dot_general x8 -> x0, matrix products: 13.8 us -> none  [product(): lax.dot_general(left, right, (((contract_left,), (contract_right,)), ((),...]
  transfers between devices with their start and end apart: 4 -> 0, of which waited for: 4 -> 0; matrix products, arithmetic and copies ran while one was open for 0% -> 0% of each run, Pallas kernels for 0% -> 0%
where the time goes in v2:
time: 108 us; the launch traced here: 107 us
  Pallas kernels  104 us (96%)
  local copies, waits for them, and re-layouts  1.91 us (2%)
    pallas_call x1, Pallas kernels, per_device(): pl.pallas_call(kernel, out_shape=(jax.ShapeDtypeStruct(basis.shape, F32),...  104 us

profile of v2, /device:TPU:6, one launch (start us, length us, event | category | flops | bytes accessed | tf_op | source)
XLA Modules:
  0.0 106.9 jit_solution(3204301075946318134)
XLA Ops:
  0.6 104.3 %shard_map.50 = (f32[16,128]{1,0:T(8,128)}, f32[32,128]{1,0:T(8,128)}) custom-call(f32[8,4,16,512]{3,2,1,0:T(8,128)} %bitcast.1, f32[16,128]{1,0:T(8,128)} %basis_hbm.1, f32[32,128]{1,0:T(8,128)} %acts_hbm.1), custom_call_target="tpu_custom_call" | custom-call | tf_op jit(solution)/shard_map/pallas_call | solution.py:255
  105.0 0.0 copy-start
  105.0 1.3 %copy.7 = f32[16,128]{1,0:T(8,128)} copy(f32[16,128]{1,0:T(8,128)} %get-tuple-element.4) | data formatting | bytes 16384
  106.3 0.0 copy-done
  106.3 0.6 copy.8
Async XLA Ops:
  105.0 1.3 %copy-start = (f32[32,128]{1,0:T(8,128)S(1)}, f32[32,128]{1,0:T(8,128)}, u32[]{:S(2)}) copy-start(f32[32,128]{1,0:T(8,128)} %get-tuple-element.5) | copy-start | bytes 49156

commit v3 on v2

--- a/solution.py
+++ b/solution.py
@@ -70,31 +70,22 @@
     y_peer = {d: freq_at(zh, step(y, d, Y), c) for d in (2, 1, 3)}
     steps = [(d, e) for d in (2, 1, 3, 0) for e in (2, 1, 3, 0) if d or e]
     xz_peer = {(d, e): frame_at(zq, step(zr, e, ZR), step(x, d, X)) for d, e in steps}
-    peers = [core_peer, zh_peer, zq_peer, *y_peer.values(), *xz_peer.values()]
+    peers = [zh_peer, zq_peer, *xz_peer.values(), *y_peer.values(), core_peer]
+
+    barrier = pltpu.get_barrier_semaphore()
+    for peer in peers:
+        pl.semaphore_signal(barrier, inc=1, device_id=peer, device_id_type=pl.DeviceIdType.MESH)
 
     loads = [
-        pltpu.make_async_copy(basis_hbm, wp.at[0, x, zq, zr], load_sem.at[0]),
-        pltpu.make_async_copy(acts_hbm, gp.at[0, c, zh, y], load_sem.at[1]),
+        pltpu.make_async_copy(acts_hbm, gp.at[0, c, zh, y], load_sem.at[0]),
+        pltpu.make_async_copy(basis_hbm, wp.at[0, x, zq, zr], load_sem.at[1]),
     ]
     for i in range(X):
         loads.append(pltpu.make_async_copy(spec_hbm.at[:, i], raw.at[i], load_sem.at[2 + i]))
     for load in loads:
         load.start()
-
-    barrier = pltpu.get_barrier_semaphore()
-    for peer in peers:
-        pl.semaphore_signal(barrier, inc=1, device_id=peer, device_id_type=pl.DeviceIdType.MESH)
-
-    for load in loads:
-        load.wait()
-    for i in range(X):
-        turned = raw[i].reshape(xbins, C * cframes).T
-        for j in range(C * ZH * Y):
-            spec_t[i, j % C, pl.ds(j // C * grows, grows)] = turned[j * grows:(j + 1) * grows]
-    for i in range(X):
-        for j in range(C):
-            spec[j, i] = spec_t[i, j].T
-
+    loads[0].wait()
+    loads[1].wait()
     pl.semaphore_wait(barrier, len(peers))
 
     copies = []
@@ -133,18 +124,23 @@
     near = send_near(mine_g)
     cross = [send(mine_g, mine_g, core_peer)]
     plane = send_plane(mine_w)
+    for load in loads[2:]:
+        load.wait()
+    for i in range(X):
+        turned = raw[i].reshape(xbins, C * cframes).T
+        for j in range(C * ZH * Y):
+            spec_t[i, j % C, pl.ds(j // C * grows, grows)] = turned[j * grows:(j + 1) * grows]
     cross += wait_near(near, lambda y_: gp.at[0, c, zh, y_])
     far_w.wait_recv()
     there = wp.at[0, x, 1 - zq, zr]
     plane_far = send_plane(there)
     far_g.wait_recv()
+    wait_all(cross)
     there = gp.at[0, c, 1 - zh, y]
     near = send_near(there)
-    cross.append(send(there, there, core_peer))
+    cross = [send(there, there, core_peer)]
     wait_all(plane.values())
     wait_all(plane_far.values())
-    cross += wait_near(near, lambda y_: gp.at[0, c, 1 - zh, y_])
-    wait_all(cross)
     plane = None
 
     def acts_terms(it, c_, zh_, xs):
@@ -160,24 +156,33 @@
         return inner(halves(spec[c_, x_] / outer(w, g)), g)
 
     for it in range(ITERS):
-        if plane is not None:
+        def add_terms(c_, zh_, xs, fresh):
+            rows = pl.ds(zh_ * Y * grows, Y * grows)
+            terms = acts_terms(it, c_, zh_, xs)
+            fcore[it, c_, rows] = terms if fresh else fcore[it, c_, rows] + terms
+
+        sides = [(1 - c, zh), (c, zh), (1 - c, 1 - zh), (c, 1 - zh)]
+        others = [step(x, d, X) for d in (1, 3, 2)]
+        if it == 0:
+            for side in sides[:2]:
+                add_terms(*side, [x, *others], True)
+            cross += wait_near(near, lambda y_: gp.at[0, c, 1 - zh, y_])
+            wait_all(cross)
+        else:
             wait_all(plane[0, e] for e in range(1, ZR))
-        for c_ in range(C):
-            for zh_ in range(ZH):
-                rows = pl.ds(zh_ * Y * grows, Y * grows)
-                fcore[it, c_, rows] = acts_terms(it, c_, zh_, [x])
-        if plane is not None:
+            for side in sides:
+                add_terms(*side, [x], True)
             wait_all(plane[at] for at in steps if at[0])
         sums = fold8(wp[it])
         for c_ in range(C):
             fcore[it, c_, pl.ds(cframes, 8)] = sums
-        others = [step(x, d, X) for d in (1, 3, 2)]
-        for c_ in (1 - c, c):
-            for zh_ in range(ZH):
-                rows = pl.ds(zh_ * Y * grows, Y * grows)
-                fcore[it, c_, rows] += acts_terms(it, c_, zh_, others)
-            if c_ is not c:
-                first = send(fcore.at[it, c_], fcore_in.at[it], core_peer)
+        for i in (2, 0, 3, 1):
+            if it:
+                add_terms(*sides[i], others, False)
+            elif i >= 2:
+                add_terms(*sides[i], [x, *others], True)
+            if i == (0 if it else 2):
+                first = send(fcore.at[it, 1 - c], fcore_in.at[it], core_peer)
         first.wait_recv()
         total = fcore[it, c] + fcore_in[it]
         for i in range(Y):
@@ -192,6 +197,10 @@
             total = total + fy_in[it, d - 1]
         fz[it] = total
         far = send(fz.at[it], fz_in.at[it], zh_peer)
+        if it == 0:
+            for i in range(X):
+                for j in range(C):
+                    spec[j, i] = spec_t[i, j].T
         far.wait_recv()
         total = total + fz_in[it]
         scale = jnp.sum(total[gpart:], axis=0)

time: 108 us -> 107 us (level)
  no operation moved by 1% of the time
where the time goes in v3:
time: 107 us
  Pallas kernels  104 us (97%)
  local copies, waits for them, and re-layouts  1.91 us (2%)
    pallas_call x1, Pallas kernels, per_device(): pl.pallas_call(kernel, out_shape=(jax.ShapeDtypeStruct(basis.shape, F32),...  104 us

profile of v3, /device:TPU:6, one launch (start us, length us, event | category | flops | bytes accessed | tf_op | source)
XLA Modules:
  0.0 106.7 jit_solution(3780356692407201153)
XLA Ops:
  0.6 104.1 %shard_map.50 = (f32[16,128]{1,0:T(8,128)}, f32[32,128]{1,0:T(8,128)}) custom-call(f32[8,4,16,512]{3,2,1,0:T(8,128)} %bitcast.1, f32[16,128]{1,0:T(8,128)} %basis_hbm.1, f32[32,128]{1,0:T(8,128)} %acts_hbm.1), custom_call_target="tpu_custom_call" | custom-call | tf_op jit(solution)/shard_map/pallas_call | solution.py:264
  104.8 0.0 copy-start
  104.8 1.3 %copy.7 = f32[16,128]{1,0:T(8,128)} copy(f32[16,128]{1,0:T(8,128)} %get-tuple-element.4) | data formatting | bytes 16384
  106.1 0.0 copy-done
  106.1 0.6 copy.8
Async XLA Ops:
  104.8 1.3 %copy-start = (f32[32,128]{1,0:T(8,128)S(1)}, f32[32,128]{1,0:T(8,128)}, u32[]{:S(2)}) copy-start(f32[32,128]{1,0:T(8,128)} %get-tuple-element.5) | copy-start | bytes 49156

commit v4 on v3

--- a/solution.py
+++ b/solution.py
@@ -10,6 +10,8 @@
 X, ZR, ZQ = 4, 4, 2
 Y, ZH, C = 4, 2, 2
 SEMS = 160
+GROUP = 2
+PAIRS = ((2, 1), (3, 0))
 F32, BF16 = jnp.float32, jnp.bfloat16
 
 
@@ -88,7 +90,12 @@
     loads[1].wait()
     pl.semaphore_wait(barrier, len(peers))
 
-    copies = []
+    copies, drained = [], []
+
+    def drain():
+        for copy in copies[len(drained):-1]:
+            copy.wait_send()
+            drained.append(copy)
 
     def send(src, dst, peer):
         slot = len(copies)
@@ -145,20 +152,22 @@
 
     def acts_terms(it, c_, zh_, xs):
         w = halves(jnp.concatenate([wp[it, i].reshape(xbins, K) for i in xs], axis=0))
-        g = halves(gp[it, c_, zh_].reshape(Y * grows, K))
-        rows = pl.ds(zh_ * Y * grows, Y * grows)
+        if zh_ is None:
+            g, rows = gp[it, c_].reshape(cframes, K), pl.ds(0, cframes)
+        else:
+            g, rows = gp[it, c_, zh_].reshape(Y * grows, K), pl.ds(zh_ * Y * grows, Y * grows)
         s = jnp.concatenate([spec_t[i, c_, rows] for i in xs], axis=1)
-        return inner(halves(s / outer(g, w)), w)
-
-    def basis_terms(it, x_, c_):
-        w = halves(wp[it, x_].reshape(xbins, K))
+        return rows, inner(halves(s / outer(halves(g), w)), w)
+
+    def basis_terms(it, xs, c_):
+        w = halves(jnp.concatenate([wp[it, i].reshape(xbins, K) for i in xs], axis=0))
         g = halves(gp[it + 1, c_].reshape(cframes, K))
-        return inner(halves(spec[c_, x_] / outer(w, g)), g)
+        s = jnp.concatenate([spec[c_, i] for i in xs], axis=0)
+        return inner(halves(s / outer(w, g)), g)
 
     for it in range(ITERS):
         def add_terms(c_, zh_, xs, fresh):
-            rows = pl.ds(zh_ * Y * grows, Y * grows)
-            terms = acts_terms(it, c_, zh_, xs)
+            rows, terms = acts_terms(it, c_, zh_, xs)
             fcore[it, c_, rows] = terms if fresh else fcore[it, c_, rows] + terms
 
         sides = [(1 - c, zh), (c, zh), (1 - c, 1 - zh), (c, 1 - zh)]
@@ -170,18 +179,18 @@
             wait_all(cross)
         else:
             wait_all(plane[0, e] for e in range(1, ZR))
-            for side in sides:
-                add_terms(*side, [x], True)
+            for c_ in (1 - c, c):
+                add_terms(c_, None, [x], True)
             wait_all(plane[at] for at in steps if at[0])
         sums = fold8(wp[it])
         for c_ in range(C):
             fcore[it, c_, pl.ds(cframes, 8)] = sums
-        for i in (2, 0, 3, 1):
+        for i in range(C):
             if it:
-                add_terms(*sides[i], others, False)
-            elif i >= 2:
-                add_terms(*sides[i], [x, *others], True)
-            if i == (0 if it else 2):
+                add_terms(sides[i][0], None, others, False)
+            else:
+                add_terms(*sides[2 + i], [x, *others], True)
+            if i == 0:
                 first = send(fcore.at[it, 1 - c], fcore_in.at[it], core_peer)
         first.wait_recv()
         total = fcore[it, c] + fcore_in[it]
@@ -197,6 +206,7 @@
             total = total + fy_in[it, d - 1]
         fz[it] = total
         far = send(fz.at[it], fz_in.at[it], zh_peer)
+        drain()
         if it == 0:
             for i in range(X):
                 for j in range(C):
@@ -212,25 +222,29 @@
             acts_out[...] = gp[it + 1, c, zh, y]
         cross += wait_near(near, lambda y_: gp.at[it + 1, c, :, y_])
 
-        for i in range(X):
-            wacc[i] = basis_terms(it, i, c)
+        for i in range(0, X, GROUP):
+            terms = basis_terms(it, range(i, i + GROUP), c)
+            for j in range(GROUP):
+                wacc[i + j] = terms[j * xbins:(j + 1) * xbins]
         sums = fold8(gp[it + 1, c])
         wait_all(cross)
         sums = sums + fold8(gp[it + 1, 1 - c])
         rs[it] = sums
         totals = {at: send(rs.at[it], rs_in.at[it, at[0], at[1]], xz_peer[at]) for at in steps}
         plane = {}
-        for d in (2, 1, 3, 0):
-            x_ = step(x, d, X)
-            terms = wacc[x_] + basis_terms(it, x_, 1 - c)
-            for i in range(ZR):
-                for j in range(ZQ):
-                    at = (j * ZR + i) * wrows
-                    rx[it, x_, i, pl.ds(j * wrows, wrows)] = terms[at:at + wrows]
-            for at in steps:
-                if at[0] == d:
-                    src = rx.at[it, x_, step(zr, at[1], ZR)]
-                    plane[at] = send(src, rx_in.at[it, at[0], at[1]], xz_peer[at])
+        for ds in PAIRS:
+            xs = [step(x, d, X) for d in ds]
+            both = basis_terms(it, xs, 1 - c)
+            for n, x_ in enumerate(xs):
+                terms = wacc[x_] + both[n * xbins:(n + 1) * xbins]
+                for i in range(ZR):
+                    for j in range(ZQ):
+                        at = (j * ZR + i) * wrows
+                        rx[it, x_, i, pl.ds(j * wrows, wrows)] = terms[at:at + wrows]
+                for at in steps:
+                    if at[0] == ds[n]:
+                        src = rx.at[it, x_, step(zr, at[1], ZR)]
+                        plane[at] = send(src, rx_in.at[it, at[0], at[1]], xz_peer[at])
         for at in steps:
             totals[at].wait_recv()
             sums = sums + rs_in[it, at[0], at[1]]
@@ -241,6 +255,7 @@
         rq[it, pl.ds(0, wpart)] = total
         rq[it, pl.ds(wpart, 8)] = sums
         far = send(rq.at[it], rq_in.at[it], zq_peer)
+        drain()
         far.wait_recv()
         total = (total + rq_in[it, pl.ds(0, wpart)]).reshape(ZQ, wrows, K)
         scale = jnp.sum(sums + rq_in[it, pl.ds(wpart, 8)], axis=0)
@@ -250,7 +265,7 @@
         else:
             basis_out[...] = wp[it + 1, x, zq, zr]
 
-    for copy in copies:
+    for copy in copies[len(drained):]:
         copy.wait_send()
 
 
@@ -264,8 +279,8 @@
     return pl.pallas_call(
         kernel,
         out_shape=(
-            jax.ShapeDtypeStruct(basis.shape, F32),
-            jax.ShapeDtypeStruct(activations.shape, F32),
+            pltpu.VMEM(basis.shape, F32),
+            pltpu.VMEM(activations.shape, F32),
         ),
         in_specs=[anywhere] * 3,
         out_specs=(vmem, vmem),
@@ -293,7 +308,7 @@
             pltpu.SemaphoreType.DMA((SEMS,)),
         ],
         compiler_params=pltpu.CompilerParams(
-            collective_id=0, has_side_effects=True, vmem_limit_bytes=67_043_328
+            collective_id=0, has_side_effects=True, vmem_limit_bytes=62914560
         ),
     )(spectrum.reshape(ZQ * ZR, X, wrows, frames), basis, activations)
 

time: 107 us -> 107 us (level); the launches traced: 107 us -> 105 us
    pallas_call x1, Pallas kernels: 104 us -> 103 us  [per_device(): pl.pallas_call(kernel, out_shape=(pltpu.VMEM(basis.shape, F32), pltpu.VME...]
where the time goes in v4:
time: 107 us; the launch traced here: 105 us
  Pallas kernels  103 us (96%)
  local copies, waits for them, and re-layouts  1.21 us (1%)
    pallas_call x1, Pallas kernels, per_device(): pl.pallas_call(kernel, out_shape=(pltpu.VMEM(basis.shape, F32), pltpu.VME...  103 us

profile of v4, /device:TPU:6, one launch (start us, length us, event | category | flops | bytes accessed | tf_op | source)
XLA Modules:
  0.0 104.8 jit_solution(16802435783327438685)
XLA Ops:
  0.6 103.0 %shard_map.50 = (f32[16,128]{1,0:T(8,128)S(1)}, f32[32,128]{1,0:T(8,128)S(1)}) custom-call(f32[8,4,16,512]{3,2,1,0:T(8,128)} %bitcast.1, f32[16,128]{1,0:T(8,128)} %basis_hbm.1, f32[32,128]{1,0:T(8,128)} %acts_hbm.1), custom_call_target="tpu_custom_call" | custom-call | tf_op jit(solution)/shard_map/pallas_call | solution.py:279
  103.6 0.6 copy.7
  104.2 0.6 copy.8

commit v5 on v4

--- a/solution.py
+++ b/solution.py
@@ -9,7 +9,7 @@
 K = 128
 X, ZR, ZQ = 4, 4, 2
 Y, ZH, C = 4, 2, 2
-SEMS = 160
+SEMS = 192
 GROUP = 2
 PAIRS = ((2, 1), (3, 0))
 F32, BF16 = jnp.float32, jnp.bfloat16
@@ -44,7 +44,7 @@
     spec_hbm, basis_hbm, acts_hbm, basis_out, acts_out,
     raw, spec, spec_t, wp, gp,
     fcore, fcore_in, fy, fy_in, fz, fz_in,
-    wacc, rx, rx_in, rs, rs_in, rq, rq_in,
+    wacc, rx, rx_in, rs, rs_in, rq, rq_in, ex, ex_in, ez, ez_in,
     load_sem, send_sem, recv_sem,
 ):
     fr = lax.axis_index("frame")
@@ -55,7 +55,7 @@
     y, zh = lax.rem(yz, Y), lax.div(yz, Y)
     wrows, grows = basis_hbm.shape[0], acts_hbm.shape[0]
     xbins, cframes = ZQ * ZR * wrows, ZH * Y * grows
-    gpart, wpart = ZH * grows, ZQ * wrows
+    wpart = ZQ * wrows
 
     def frame_at(zq_, zr_, x_):
         return ((zq_ * ZR + zr_) * X + x_, fq)
@@ -92,8 +92,8 @@
 
     copies, drained = [], []
 
-    def drain():
-        for copy in copies[len(drained):-1]:
+    def drain(last):
+        for copy in copies[len(drained):-last]:
             copy.wait_send()
             drained.append(copy)
 
@@ -144,7 +144,7 @@
     far_g.wait_recv()
     wait_all(cross)
     there = gp.at[0, c, 1 - zh, y]
-    near = send_near(there)
+    far_near = send_near(there)
     cross = [send(there, there, core_peer)]
     wait_all(plane.values())
     wait_all(plane_far.values())
@@ -157,7 +157,7 @@
         else:
             g, rows = gp[it, c_, zh_].reshape(Y * grows, K), pl.ds(zh_ * Y * grows, Y * grows)
         s = jnp.concatenate([spec_t[i, c_, rows] for i in xs], axis=1)
-        return rows, inner(halves(s / outer(halves(g), w)), w)
+        return inner(halves(s / outer(halves(g), w)), w)
 
     def basis_terms(it, xs, c_):
         w = halves(jnp.concatenate([wp[it, i].reshape(xbins, K) for i in xs], axis=0))
@@ -165,62 +165,94 @@
         s = jnp.concatenate([spec[c_, i] for i in xs], axis=0)
         return inner(halves(s / outer(w, g)), g)
 
+    half, tail = Y * grows, pl.ds(grows, 8)
+
     for it in range(ITERS):
-        def add_terms(c_, zh_, xs, fresh):
-            rows, terms = acts_terms(it, c_, zh_, xs)
-            fcore[it, c_, rows] = terms if fresh else fcore[it, c_, rows] + terms
-
-        sides = [(1 - c, zh), (c, zh), (1 - c, 1 - zh), (c, 1 - zh)]
+        order = (0, 1) if it else (zh, 1 - zh)
+        arrival = (0, 1) if it else (1 - zh, zh)
         others = [step(x, d, X) for d in (1, 3, 2)]
-        if it == 0:
-            for side in sides[:2]:
-                add_terms(*side, [x, *others], True)
-            cross += wait_near(near, lambda y_: gp.at[0, c, 1 - zh, y_])
-            wait_all(cross)
-        else:
+
+        def add_terms(c_, k, xs):
+            terms = acts_terms(it, c_, order[k], xs)
+            rows = pl.ds(0, half)
+            fcore[it, c_, order[k], rows] = fcore[it, c_, order[k], rows] + terms if it else terms
+
+        def send_core(k):
+            rows = pl.ds(0, half if k else half + 8)
+            return send(fcore.at[it, 1 - c, order[k], rows], fcore_in.at[it, order[k], rows], core_peer)
+
+        def send_y(k, core):
+            h, n = order[k], grows if k else grows + 8
+            core.wait_recv()
+            for i in range(Y):
+                rows = pl.ds(i * grows, grows)
+                fy[it, h, i, pl.ds(0, grows)] = fcore[it, c, h, rows] + fcore_in[it, h, rows]
+                if k == 0:
+                    rows = pl.ds(half, 8)
+                    fy[it, h, i, tail] = fcore[it, c, h, rows] + fcore_in[it, h, rows]
+            rows = pl.ds(0, n)
+            return {
+                d: send(fy.at[it, h, step(y, d, Y), rows], fy_in.at[it, h, d - 1, rows], y_peer[d])
+                for d in (2, 1, 3)
+            }
+
+        def send_far(k, near):
+            h, rows = order[k], pl.ds(0, grows if k else grows + 8)
+            total = fy[it, h, y, rows]
+            for d in (1, 3, 2):
+                near[d].wait_recv()
+                total = total + fy_in[it, h, d - 1, rows]
+            fz[it, h, rows] = total
+            return send(fz.at[it, h, rows], fz_in.at[it, h, rows], zh_peer)
+
+        if it:
             wait_all(plane[0, e] for e in range(1, ZR))
             for c_ in (1 - c, c):
-                add_terms(c_, None, [x], True)
+                terms = acts_terms(it, c_, None, [x])
+                for i in range(ZH):
+                    fcore[it, c_, i, pl.ds(0, half)] = terms[i * half:(i + 1) * half]
             wait_all(plane[at] for at in steps if at[0])
         sums = fold8(wp[it])
         for c_ in range(C):
-            fcore[it, c_, pl.ds(cframes, 8)] = sums
-        for i in range(C):
-            if it:
-                add_terms(sides[i][0], None, others, False)
-            else:
-                add_terms(*sides[2 + i], [x, *others], True)
-            if i == 0:
-                first = send(fcore.at[it, 1 - c], fcore_in.at[it], core_peer)
-        first.wait_recv()
-        total = fcore[it, c] + fcore_in[it]
-        for i in range(Y):
-            for j in range(ZH):
-                at = (j * Y + i) * grows
-                fy[it, i, pl.ds(j * grows, grows)] = total[at:at + grows]
-            fy[it, i, pl.ds(gpart, 8)] = total[cframes:]
-        near = {d: send(fy.at[it, step(y, d, Y)], fy_in.at[it, d - 1], y_peer[d]) for d in (2, 1, 3)}
-        total = fy[it, y]
-        for d in (1, 3, 2):
-            near[d].wait_recv()
-            total = total + fy_in[it, d - 1]
-        fz[it] = total
-        far = send(fz.at[it], fz_in.at[it], zh_peer)
-        drain()
+            fcore[it, c_, order[0], pl.ds(half, 8)] = sums
+        xs = others if it else [x, *others]
+        add_terms(1 - c, 0, xs)
+        core = [send_core(0)]
+        add_terms(c, 0, xs)
+        if it:
+            add_terms(1 - c, 1, xs)
+            core.append(send_core(1))
+            near = [send_y(0, core[0])]
+            add_terms(c, 1, xs)
+        else:
+            cross += wait_near(far_near, lambda y_: gp.at[0, c, 1 - zh, y_])
+            near = [send_y(0, core[0])]
+            wait_all(cross)
+            add_terms(1 - c, 1, xs)
+            core.append(send_core(1))
+            add_terms(c, 1, xs)
+        near.append(send_y(1, core[1]))
+        far = [send_far(k, near[k]) for k in range(ZH)]
+        drain(ZH)
         if it == 0:
             for i in range(X):
                 for j in range(C):
                     spec[j, i] = spec_t[i, j].T
-        far.wait_recv()
-        total = total + fz_in[it]
-        scale = jnp.sum(total[gpart:], axis=0)
-        gp[it + 1, c, :, y] = gp[it, c, :, y] * total[:gpart].reshape(ZH, grows, K) / scale
-        mine = gp.at[it + 1, c, :, y]
-        near = send_near(mine)
-        cross = [send(mine, mine, core_peer)]
+        near, cross = [], []
+        for k in range(ZH):
+            far[k].wait_recv()
+            h = arrival[k]
+            if k == 0:
+                scale = jnp.sum(fz[it, order[0], tail] + fz_in[it, h, tail], axis=0)
+            rows = pl.ds(0, grows)
+            gp[it + 1, c, h, y] = gp[it, c, h, y] * (fz[it, h, rows] + fz_in[it, h, rows]) / scale
+            mine = gp.at[it + 1, c, h, y]
+            near.append(send_near(mine))
+            cross.append(send(mine, mine, core_peer))
         if it + 1 == ITERS:
             acts_out[...] = gp[it + 1, c, zh, y]
-        cross += wait_near(near, lambda y_: gp.at[it + 1, c, :, y_])
+        for k in range(ZH):
+            cross += wait_near(near[k], lambda y_: gp.at[it + 1, c, arrival[k], y_])
 
         for i in range(0, X, GROUP):
             terms = basis_terms(it, range(i, i + GROUP), c)
@@ -237,33 +269,56 @@
             both = basis_terms(it, xs, 1 - c)
             for n, x_ in enumerate(xs):
                 terms = wacc[x_] + both[n * xbins:(n + 1) * xbins]
+                if it + 1 == ITERS:
+                    ex[x_] = terms
+                    if ds[n]:
+                        plane[ds[n]] = send(ex.at[x_], ex_in.at[ds[n] - 1], xz_peer[ds[n], 0])
+                    continue
                 for i in range(ZR):
                     for j in range(ZQ):
                         at = (j * ZR + i) * wrows
-                        rx[it, x_, i, pl.ds(j * wrows, wrows)] = terms[at:at + wrows]
+                        rx[x_, i, pl.ds(j * wrows, wrows)] = terms[at:at + wrows]
                 for at in steps:
                     if at[0] == ds[n]:
-                        src = rx.at[it, x_, step(zr, at[1], ZR)]
-                        plane[at] = send(src, rx_in.at[it, at[0], at[1]], xz_peer[at])
+                        src = rx.at[x_, step(zr, at[1], ZR)]
+                        plane[at] = send(src, rx_in.at[at[0], at[1]], xz_peer[at])
         for at in steps:
             totals[at].wait_recv()
             sums = sums + rs_in[it, at[0], at[1]]
-        total = rx[it, x, zr]
+        rq[it, pl.ds(wpart, 8)] = sums
+        if it + 1 == ITERS:
+            rows = pl.ds(wpart, 8)
+            far = send(rq.at[it, rows], rq_in.at[it, rows], zq_peer)
+            total = ex[x]
+            for d in (1, 3, 2):
+                plane[d].wait_recv()
+                total = total + ex_in[d - 1]
+            ez[...] = total.reshape(ZQ * ZR, wrows, K)
+            parts = {}
+            for d in (4, 3, 5, 2, 6, 1, 7):
+                there = step(zl, d, ZQ * ZR)
+                parts[d] = send(ez.at[there], ez_in.at[d - 1], (there * X + x, fq))
+            drain(ZQ * ZR)
+            far.wait_recv()
+            scale = jnp.sum(sums + rq_in[it, rows], axis=0)
+            total = ez[zl]
+            for d in (1, 7, 2, 6, 3, 5, 4):
+                parts[d].wait_recv()
+                total = total + ez_in[d - 1]
+            basis_out[...] = wp[it, x, zq, zr] * total / scale
+            continue
+        total = rx[x, zr]
         for at in sorted(steps):
             plane[at].wait_recv()
-            total = total + rx_in[it, at[0], at[1]]
+            total = total + rx_in[at[0], at[1]]
         rq[it, pl.ds(0, wpart)] = total
-        rq[it, pl.ds(wpart, 8)] = sums
         far = send(rq.at[it], rq_in.at[it], zq_peer)
-        drain()
+        drain(1)
         far.wait_recv()
         total = (total + rq_in[it, pl.ds(0, wpart)]).reshape(ZQ, wrows, K)
         scale = jnp.sum(sums + rq_in[it, pl.ds(wpart, 8)], axis=0)
         wp[it + 1, x, :, zr] = wp[it, x, :, zr] * total / scale
-        if it + 1 < ITERS:
-            plane = send_plane(wp.at[it + 1, x, :, zr])
-        else:
-            basis_out[...] = wp[it + 1, x, zq, zr]
+        plane = send_plane(wp.at[it + 1, x, :, zr])
 
     for copy in copies[len(drained):]:
         copy.wait_send()
@@ -272,8 +327,7 @@
 def per_device(spectrum, basis, activations):
     bins, frames = spectrum.shape
     wrows, grows = basis.shape[0], activations.shape[0]
-    gpart, wpart = ZH * grows, ZQ * wrows
-    fwide = Y * gpart + 8
+    wpart = ZQ * wrows
     anywhere = pl.BlockSpec(memory_space=pl.ANY)
     vmem = pl.BlockSpec(memory_space=pltpu.VMEM)
     return pl.pallas_call(
@@ -290,19 +344,23 @@
             pltpu.VMEM((X, C, frames // C, bins // X), F32),
             pltpu.VMEM((ITERS + 1, X, ZQ, ZR, wrows, K), F32),
             pltpu.VMEM((ITERS + 1, C, ZH, Y, grows, K), F32),
-            pltpu.VMEM((ITERS, C, fwide, K), F32),
-            pltpu.VMEM((ITERS, fwide, K), F32),
-            pltpu.VMEM((ITERS, Y, gpart + 8, K), F32),
-            pltpu.VMEM((ITERS, Y - 1, gpart + 8, K), F32),
-            pltpu.VMEM((ITERS, gpart + 8, K), F32),
-            pltpu.VMEM((ITERS, gpart + 8, K), F32),
+            pltpu.VMEM((ITERS, C, ZH, Y * grows + 8, K), F32),
+            pltpu.VMEM((ITERS, ZH, Y * grows + 8, K), F32),
+            pltpu.VMEM((ITERS, ZH, Y, grows + 8, K), F32),
+            pltpu.VMEM((ITERS, ZH, Y - 1, grows + 8, K), F32),
+            pltpu.VMEM((ITERS, ZH, grows + 8, K), F32),
+            pltpu.VMEM((ITERS, ZH, grows + 8, K), F32),
             pltpu.VMEM((X, bins // X, K), F32),
-            pltpu.VMEM((ITERS, X, ZR, wpart, K), F32),
-            pltpu.VMEM((ITERS, X, ZR, wpart, K), F32),
+            pltpu.VMEM((X, ZR, wpart, K), F32),
+            pltpu.VMEM((X, ZR, wpart, K), F32),
             pltpu.VMEM((ITERS, 8, K), F32),
             pltpu.VMEM((ITERS, X, ZR, 8, K), F32),
             pltpu.VMEM((ITERS, wpart + 8, K), F32),
             pltpu.VMEM((ITERS, wpart + 8, K), F32),
+            pltpu.VMEM((X, bins // X, K), F32),
+            pltpu.VMEM((X - 1, bins // X, K), F32),
+            pltpu.VMEM((ZQ * ZR, wrows, K), F32),
+            pltpu.VMEM((ZQ * ZR - 1, wrows, K), F32),
             pltpu.SemaphoreType.DMA((2 + X,)),
             pltpu.SemaphoreType.DMA((SEMS,)),
             pltpu.SemaphoreType.DMA((SEMS,)),

time: 107 us -> 103 us (0.963)
  Pallas kernels: 103 us -> 99.7 us
    pallas_call x1, Pallas kernels: 103 us -> 99.7 us  [per_device(): pl.pallas_call(kernel, out_shape=(pltpu.VMEM(basis.shape, F32), pltpu.VME...]
where the time goes in v5:
time: 103 us; the launch traced here: 102 us
  Pallas kernels  99.7 us (97%)
  local copies, waits for them, and re-layouts  1.21 us (1%)
    pallas_call x1, Pallas kernels, per_device(): pl.pallas_call(kernel, out_shape=(pltpu.VMEM(basis.shape, F32), pltpu.VME...  99.7 us

profile of v5, /device:TPU:6, one launch (start us, length us, event | category | flops | bytes accessed | tf_op | source)
XLA Modules:
  0.0 101.5 jit_solution(6175267942915966952)
XLA Ops:
  0.6 99.7 %shard_map.50 = (f32[16,128]{1,0:T(8,128)S(1)}, f32[32,128]{1,0:T(8,128)S(1)}) custom-call(f32[8,4,16,512]{3,2,1,0:T(8,128)} %bitcast.1, f32[16,128]{1,0:T(8,128)} %basis_hbm.1, f32[32,128]{1,0:T(8,128)} %acts_hbm.1), custom_call_target="tpu_custom_call" | custom-call | tf_op jit(solution)/shard_map/pallas_call | solution.py:333
  100.3 0.6 copy.7
  100.9 0.6 copy.8

commit v6 on v5

--- a/solution.py
+++ b/solution.py
@@ -9,7 +9,7 @@
 K = 128
 X, ZR, ZQ = 4, 4, 2
 Y, ZH, C = 4, 2, 2
-SEMS = 192
+SEMS = 224
 GROUP = 2
 PAIRS = ((2, 1), (3, 0))
 F32, BF16 = jnp.float32, jnp.bfloat16
@@ -44,7 +44,7 @@
     spec_hbm, basis_hbm, acts_hbm, basis_out, acts_out,
     raw, spec, spec_t, wp, gp,
     fcore, fcore_in, fy, fy_in, fz, fz_in,
-    wacc, rx, rx_in, rs, rs_in, rq, rq_in, ex, ex_in, ez, ez_in,
+    wacc, rx, rx_in, rt, rs, rs_in, rq, rq_in, ex_in, ez, ez_in,
     load_sem, send_sem, recv_sem,
 ):
     fr = lax.axis_index("frame")
@@ -55,7 +55,6 @@
     y, zh = lax.rem(yz, Y), lax.div(yz, Y)
     wrows, grows = basis_hbm.shape[0], acts_hbm.shape[0]
     xbins, cframes = ZQ * ZR * wrows, ZH * Y * grows
-    wpart = ZQ * wrows
 
     def frame_at(zq_, zr_, x_):
         return ((zq_ * ZR + zr_) * X + x_, fq)
@@ -206,31 +205,32 @@
             return send(fz.at[it, h, rows], fz_in.at[it, h, rows], zh_peer)
 
         if it:
-            wait_all(plane[0, e] for e in range(1, ZR))
+            wait_all(part[0, e] for part in plane_parts for e in range(1, ZR))
             for c_ in (1 - c, c):
                 terms = acts_terms(it, c_, None, [x])
                 for i in range(ZH):
                     fcore[it, c_, i, pl.ds(0, half)] = terms[i * half:(i + 1) * half]
-            wait_all(plane[at] for at in steps if at[0])
+            wait_all(part[at] for part in plane_parts for at in steps if at[0])
         sums = fold8(wp[it])
         for c_ in range(C):
             fcore[it, c_, order[0], pl.ds(half, 8)] = sums
         xs = others if it else [x, *others]
         add_terms(1 - c, 0, xs)
         core = [send_core(0)]
-        add_terms(c, 0, xs)
         if it:
             add_terms(1 - c, 1, xs)
             core.append(send_core(1))
+            add_terms(c, 0, xs)
             near = [send_y(0, core[0])]
             add_terms(c, 1, xs)
         else:
+            add_terms(c, 0, xs)
             cross += wait_near(far_near, lambda y_: gp.at[0, c, 1 - zh, y_])
             near = [send_y(0, core[0])]
+            add_terms(c, 1, xs)
             wait_all(cross)
             add_terms(1 - c, 1, xs)
             core.append(send_core(1))
-            add_terms(c, 1, xs)
         near.append(send_y(1, core[1]))
         far = [send_far(k, near[k]) for k in range(ZH)]
         drain(ZH)
@@ -261,64 +261,69 @@
         sums = fold8(gp[it + 1, c])
         wait_all(cross)
         sums = sums + fold8(gp[it + 1, 1 - c])
-        rs[it] = sums
-        totals = {at: send(rs.at[it], rs_in.at[it, at[0], at[1]], xz_peer[at]) for at in steps}
+        rt[it] = sums
+        totals = {at: send(rt.at[it], rs_in.at[it, at[0], at[1]], xz_peer[at]) for at in steps}
         plane = {}
+        sides = (1 - zq, zq) if it + 1 == ITERS else range(ZQ)
         for ds in PAIRS:
             xs = [step(x, d, X) for d in ds]
             both = basis_terms(it, xs, 1 - c)
             for n, x_ in enumerate(xs):
                 terms = wacc[x_] + both[n * xbins:(n + 1) * xbins]
-                if it + 1 == ITERS:
-                    ex[x_] = terms
-                    if ds[n]:
-                        plane[ds[n]] = send(ex.at[x_], ex_in.at[ds[n] - 1], xz_peer[ds[n], 0])
-                    continue
-                for i in range(ZR):
-                    for j in range(ZQ):
-                        at = (j * ZR + i) * wrows
-                        rx[x_, i, pl.ds(j * wrows, wrows)] = terms[at:at + wrows]
-                for at in steps:
-                    if at[0] == ds[n]:
-                        src = rx.at[x_, step(zr, at[1], ZR)]
-                        plane[at] = send(src, rx_in.at[at[0], at[1]], xz_peer[at])
+                rx[it, x_] = terms.reshape(ZQ, ZR, wrows, K)
+            for k, j in enumerate(sides):
+                for d, x_ in zip(ds, xs):
+                    if it + 1 < ITERS:
+                        for at in steps:
+                            if at[0] == d:
+                                src = rx.at[it, x_, j, step(zr, at[1], ZR)]
+                                plane[k, at] = send(src, rx_in.at[at[0], j, at[1]], xz_peer[at])
+                    elif d:
+                        plane[k, d] = send(rx.at[it, x_, j], ex_in.at[d - 1, j], xz_peer[d, 0])
         for at in steps:
             totals[at].wait_recv()
             sums = sums + rs_in[it, at[0], at[1]]
-        rq[it, pl.ds(wpart, 8)] = sums
-        if it + 1 == ITERS:
-            rows = pl.ds(wpart, 8)
-            far = send(rq.at[it, rows], rq_in.at[it, rows], zq_peer)
-            total = ex[x]
-            for d in (1, 3, 2):
-                plane[d].wait_recv()
-                total = total + ex_in[d - 1]
-            ez[...] = total.reshape(ZQ * ZR, wrows, K)
+        rs[it] = sums
+        swap = send(rs.at[it], rs_in.at[it, 0, 0], zq_peer)
+        if it + 1 < ITERS:
+            far = []
+            for j in range(ZQ):
+                total = rx[it, x, j, zr]
+                for at in sorted(steps):
+                    plane[j, at].wait_recv()
+                    total = total + rx_in[at[0], j, at[1]]
+                rq[j] = total
+                far.append(send(rq.at[j], rq_in.at[j], zq_peer))
+            drain(1 + ZQ)
+            swap.wait_recv()
+            scale = jnp.sum(sums + rs_in[it, 0, 0], axis=0)
+            plane_parts = []
+            for j in range(ZQ):
+                far[j].wait_recv()
+                wp[it + 1, x, j, zr] = wp[it, x, j, zr] * (rq[j] + rq_in[j]) / scale
+                plane_parts.append(send_plane(wp.at[it + 1, x, j, zr]))
+        else:
             parts = {}
-            for d in (4, 3, 5, 2, 6, 1, 7):
-                there = step(zl, d, ZQ * ZR)
-                parts[d] = send(ez.at[there], ez_in.at[d - 1], (there * X + x, fq))
+            for k, j in enumerate(sides):
+                total = rx[it, x, j]
+                for d in (1, 3, 2):
+                    plane[k, d].wait_recv()
+                    total = total + ex_in[d - 1, j]
+                ez[j] = total
+                for e in (2, 1, 3, 0):
+                    if e or k == 0:
+                        there = step(zr, e, ZR)
+                        parts[k, e] = send(ez.at[j, there], ez_in.at[k, e], frame_at(j, there, x))
             drain(ZQ * ZR)
-            far.wait_recv()
-            scale = jnp.sum(sums + rq_in[it, rows], axis=0)
-            total = ez[zl]
-            for d in (1, 7, 2, 6, 3, 5, 4):
-                parts[d].wait_recv()
-                total = total + ez_in[d - 1]
+            swap.wait_recv()
+            scale = jnp.sum(sums + rs_in[it, 0, 0], axis=0)
+            total = ez[zq, zr]
+            for k in (1, 0):
+                for e in (1, 3, 2, 0):
+                    if e or k == 0:
+                        parts[k, e].wait_recv()
+                        total = total + ez_in[k, e]
             basis_out[...] = wp[it, x, zq, zr] * total / scale
-            continue
-        total = rx[x, zr]
-        for at in sorted(steps):
-            plane[at].wait_recv()
-            total = total + rx_in[at[0], at[1]]
-        rq[it, pl.ds(0, wpart)] = total
-        far = send(rq.at[it], rq_in.at[it], zq_peer)
-        drain(1)
-        far.wait_recv()
-        total = (total + rq_in[it, pl.ds(0, wpart)]).reshape(ZQ, wrows, K)
-        scale = jnp.sum(sums + rq_in[it, pl.ds(wpart, 8)], axis=0)
-        wp[it + 1, x, :, zr] = wp[it, x, :, zr] * total / scale
-        plane = send_plane(wp.at[it + 1, x, :, zr])
 
     for copy in copies[len(drained):]:
         copy.wait_send()
@@ -327,7 +332,6 @@
 def per_device(spectrum, basis, activations):
     bins, frames = spectrum.shape
     wrows, grows = basis.shape[0], activations.shape[0]
-    wpart = ZQ * wrows
     anywhere = pl.BlockSpec(memory_space=pl.ANY)
     vmem = pl.BlockSpec(memory_space=pltpu.VMEM)
     return pl.pallas_call(
@@ -351,16 +355,16 @@
             pltpu.VMEM((ITERS, ZH, grows + 8, K), F32),
             pltpu.VMEM((ITERS, ZH, grows + 8, K), F32),
             pltpu.VMEM((X, bins // X, K), F32),
-            pltpu.VMEM((X, ZR, wpart, K), F32),
-            pltpu.VMEM((X, ZR, wpart, K), F32),
+            pltpu.VMEM((ITERS, X, ZQ, ZR, wrows, K), F32),
+            pltpu.VMEM((X, ZQ, ZR, wrows, K), F32),
+            pltpu.VMEM((ITERS, 8, K), F32),
             pltpu.VMEM((ITERS, 8, K), F32),
             pltpu.VMEM((ITERS, X, ZR, 8, K), F32),
-            pltpu.VMEM((ITERS, wpart + 8, K), F32),
-            pltpu.VMEM((ITERS, wpart + 8, K), F32),
-            pltpu.VMEM((X, bins // X, K), F32),
-            pltpu.VMEM((X - 1, bins // X, K), F32),
-            pltpu.VMEM((ZQ * ZR, wrows, K), F32),
-            pltpu.VMEM((ZQ * ZR - 1, wrows, K), F32),
+            pltpu.VMEM((ZQ, wrows, K), F32),
+            pltpu.VMEM((ZQ, wrows, K), F32),
+            pltpu.VMEM((X - 1, ZQ, ZR, wrows, K), F32),
+            pltpu.VMEM((ZQ, ZR, wrows, K), F32),
+            pltpu.VMEM((ZQ, ZR, wrows, K), F32),
             pltpu.SemaphoreType.DMA((2 + X,)),
             pltpu.SemaphoreType.DMA((SEMS,)),
             pltpu.SemaphoreType.DMA((SEMS,)),

time: 103 us -> 102 us (level)
  no operation moved by 1% of the time
where the time goes in v6:
time: 102 us; the launch traced here: 101 us
  Pallas kernels  99.6 us (98%)
  local copies, waits for them, and re-layouts  1.21 us (1%)
    pallas_call x1, Pallas kernels, per_device(): pl.pallas_call(kernel, out_shape=(pltpu.VMEM(basis.shape, F32), pltpu.VME...  99.6 us

profile of v6, /device:TPU:6, one launch (start us, length us, event | category | flops | bytes accessed | tf_op | source)
XLA Modules:
  0.0 101.4 jit_solution(5236891070776247416)
XLA Ops:
  0.6 99.6 %shard_map.50 = (f32[16,128]{1,0:T(8,128)S(1)}, f32[32,128]{1,0:T(8,128)S(1)}) custom-call(f32[8,4,16,512]{3,2,1,0:T(8,128)} %bitcast.1, f32[16,128]{1,0:T(8,128)} %basis_hbm.1, f32[32,128]{1,0:T(8,128)} %acts_hbm.1), custom_call_target="tpu_custom_call" | custom-call | tf_op jit(solution)/shard_map/pallas_call | solution.py:337
  100.2 0.6 copy.7
  100.8 0.6 copy.8

commit v7 on v6

--- a/solution.py
+++ b/solution.py
@@ -146,8 +146,8 @@
     far_near = send_near(there)
     cross = [send(there, there, core_peer)]
     wait_all(plane.values())
+    cross += wait_near(far_near, lambda y_: gp.at[0, c, 1 - zh, y_])
     wait_all(plane_far.values())
-    plane = None
 
     def acts_terms(it, c_, zh_, xs):
         w = halves(jnp.concatenate([wp[it, i].reshape(xbins, K) for i in xs], axis=0))
@@ -225,12 +225,11 @@
             add_terms(c, 1, xs)
         else:
             add_terms(c, 0, xs)
-            cross += wait_near(far_near, lambda y_: gp.at[0, c, 1 - zh, y_])
-            near = [send_y(0, core[0])]
-            add_terms(c, 1, xs)
             wait_all(cross)
             add_terms(1 - c, 1, xs)
             core.append(send_core(1))
+            near = [send_y(0, core[0])]
+            add_terms(c, 1, xs)
         near.append(send_y(1, core[1]))
         far = [send_far(k, near[k]) for k in range(ZH)]
         drain(ZH)
@@ -329,12 +328,23 @@
         copy.wait_send()
 
 
+def write_out(basis_ref, acts_ref, basis_out, acts_out, sems):
+    copies = [
+        pltpu.make_async_copy(basis_ref, basis_out, sems.at[0]),
+        pltpu.make_async_copy(acts_ref, acts_out, sems.at[1]),
+    ]
+    for copy in copies:
+        copy.start()
+    for copy in copies:
+        copy.wait()
+
+
 def per_device(spectrum, basis, activations):
     bins, frames = spectrum.shape
     wrows, grows = basis.shape[0], activations.shape[0]
     anywhere = pl.BlockSpec(memory_space=pl.ANY)
     vmem = pl.BlockSpec(memory_space=pltpu.VMEM)
-    return pl.pallas_call(
+    fresh = pl.pallas_call(
         kernel,
         out_shape=(
             pltpu.VMEM(basis.shape, F32),
@@ -373,6 +383,17 @@
             collective_id=0, has_side_effects=True, vmem_limit_bytes=62914560
         ),
     )(spectrum.reshape(ZQ * ZR, X, wrows, frames), basis, activations)
+    return pl.pallas_call(
+        write_out,
+        out_shape=(
+            jax.ShapeDtypeStruct(basis.shape, F32),
+            jax.ShapeDtypeStruct(activations.shape, F32),
+        ),
+        in_specs=[vmem, vmem],
+        out_specs=(anywhere, anywhere),
+        scratch_shapes=[pltpu.SemaphoreType.DMA((2,))],
+        compiler_params=pltpu.CompilerParams(vmem_limit_bytes=1 << 20),
+    )(*fresh)
 
 
 def solution(mesh):

time: 102 us -> 100 us (0.980)
  local copies, waits for them, and re-layouts: 1.21 us -> 0 us
    unnamed x2 -> x0, local copies, waits for them, and re-layouts: 1.21 us -> none
where the time goes in v7:
time: 100 us
  Pallas kernels  99.4 us (99%)
    pallas_call x1, Pallas kernels, per_device(): pl.pallas_call(kernel, out_shape=(pltpu.VMEM(basis.shape, F32), pltpu.VME...  98.8 us

profile of v7, /device:TPU:6, one launch (start us, length us, event | category | flops | bytes accessed | tf_op | source)
XLA Modules:
  0.0 100.1 jit_solution(6828102928677273579)
XLA Ops:
  0.6 98.8 %shard_map.50 = (f32[16,128]{1,0:T(8,128)S(1)}, f32[32,128]{1,0:T(8,128)S(1)}) custom-call(f32[8,4,16,512]{3,2,1,0:T(8,128)} %bitcast.1, f32[16,128]{1,0:T(8,128)} %basis_hbm.1, f32[32,128]{1,0:T(8,128)} %acts_hbm.1), custom_call_target="tpu_custom_call" | custom-call | tf_op jit(solution)/shard_map/pallas_call | solution.py:347
  99.5 0.6 shard_map.51

commit v8 on v7

--- a/solution.py
+++ b/solution.py
@@ -67,11 +67,12 @@
 
     core_peer = freq_at(zh, y, 1 - c)
     zh_peer = freq_at(1 - zh, y, c)
+    zh_other = freq_at(1 - zh, y, 1 - c)
     zq_peer = frame_at(1 - zq, zr, x)
     y_peer = {d: freq_at(zh, step(y, d, Y), c) for d in (2, 1, 3)}
     steps = [(d, e) for d in (2, 1, 3, 0) for e in (2, 1, 3, 0) if d or e]
     xz_peer = {(d, e): frame_at(zq, step(zr, e, ZR), step(x, d, X)) for d, e in steps}
-    peers = [zh_peer, zq_peer, *xz_peer.values(), *y_peer.values(), core_peer]
+    peers = [zh_peer, zh_other, zq_peer, *xz_peer.values(), *y_peer.values(), core_peer]
 
     barrier = pltpu.get_barrier_semaphore()
     for peer in peers:
@@ -125,7 +126,7 @@
         return passed
 
     mine_w, mine_g = wp.at[0, x, zq, zr], gp.at[0, c, zh, y]
-    far_g = send(mine_g, mine_g, zh_peer)
+    far_g = [send(mine_g, mine_g, zh_peer), send(mine_g, mine_g, zh_other)]
     far_w = send(mine_w, mine_w, zq_peer)
     near = send_near(mine_g)
     cross = [send(mine_g, mine_g, core_peer)]
@@ -140,13 +141,10 @@
     far_w.wait_recv()
     there = wp.at[0, x, 1 - zq, zr]
     plane_far = send_plane(there)
-    far_g.wait_recv()
+    wait_all(far_g)
+    far_near = send_near(gp.at[0, :, 1 - zh, y])
+    wait_all(plane.values())
     wait_all(cross)
-    there = gp.at[0, c, 1 - zh, y]
-    far_near = send_near(there)
-    cross = [send(there, there, core_peer)]
-    wait_all(plane.values())
-    cross += wait_near(far_near, lambda y_: gp.at[0, c, 1 - zh, y_])
     wait_all(plane_far.values())
 
     def acts_terms(it, c_, zh_, xs):
@@ -225,7 +223,7 @@
             add_terms(c, 1, xs)
         else:
             add_terms(c, 0, xs)
-            wait_all(cross)
+            wait_all(far_near.values())
             add_terms(1 - c, 1, xs)
             core.append(send_core(1))
             near = [send_y(0, core[0])]
@@ -259,9 +257,6 @@
                 wacc[i + j] = terms[j * xbins:(j + 1) * xbins]
         sums = fold8(gp[it + 1, c])
         wait_all(cross)
-        sums = sums + fold8(gp[it + 1, 1 - c])
-        rt[it] = sums
-        totals = {at: send(rt.at[it], rs_in.at[it, at[0], at[1]], xz_peer[at]) for at in steps}
         plane = {}
         sides = (1 - zq, zq) if it + 1 == ITERS else range(ZQ)
         for ds in PAIRS:
@@ -279,6 +274,10 @@
                                 plane[k, at] = send(src, rx_in.at[at[0], j, at[1]], xz_peer[at])
                     elif d:
                         plane[k, d] = send(rx.at[it, x_, j], ex_in.at[d - 1, j], xz_peer[d, 0])
+            if ds is PAIRS[0]:
+                sums = sums + fold8(gp[it + 1, 1 - c])
+                rt[it] = sums
+                totals = {at: send(rt.at[it], rs_in.at[it, at[0], at[1]], xz_peer[at]) for at in steps}
         for at in steps:
             totals[at].wait_recv()
             sums = sums + rs_in[it, at[0], at[1]]

time: 100 us -> 105 us (1.050); the launches traced: 100 us -> 103 us
  Pallas kernels: 99.4 us -> 102 us
    pallas_call x1, Pallas kernels: 98.8 us -> 102 us  [per_device(): pl.pallas_call(kernel, out_shape=(pltpu.VMEM(basis.shape, F32), pltpu.VME...]
where the time goes in v8:
time: 105 us; the launch traced here: 103 us
  Pallas kernels  102 us (97%)
    pallas_call x1, Pallas kernels, per_device(): pl.pallas_call(kernel, out_shape=(pltpu.VMEM(basis.shape, F32), pltpu.VME...  102 us

profile of v8, /device:TPU:6, one launch (start us, length us, event | category | flops | bytes accessed | tf_op | source)
XLA Modules:
  0.0 103.0 jit_solution(6874070563848994882)
XLA Ops:
  0.6 101.7 %shard_map.50 = (f32[16,128]{1,0:T(8,128)S(1)}, f32[32,128]{1,0:T(8,128)S(1)}) custom-call(f32[8,4,16,512]{3,2,1,0:T(8,128)} %bitcast.1, f32[16,128]{1,0:T(8,128)} %basis_hbm.1, f32[32,128]{1,0:T(8,128)} %acts_hbm.1), custom_call_target="tpu_custom_call" | custom-call | tf_op jit(solution)/shard_map/pallas_call | solution.py:346
  102.3 0.6 shard_map.51

commit v9 on v7

--- a/solution.py
+++ b/solution.py
@@ -9,7 +9,7 @@
 K = 128
 X, ZR, ZQ = 4, 4, 2
 Y, ZH, C = 4, 2, 2
-SEMS = 224
+SEMS = 240
 GROUP = 2
 PAIRS = ((2, 1), (3, 0))
 F32, BF16 = jnp.float32, jnp.bfloat16
@@ -43,7 +43,7 @@
 def kernel(
     spec_hbm, basis_hbm, acts_hbm, basis_out, acts_out,
     raw, spec, spec_t, wp, gp,
-    fcore, fcore_in, fy, fy_in, fz, fz_in,
+    st, st_in, su, su_in, fcore, fcore_in, fy, fy_in, fz, fz_in,
     wacc, rx, rx_in, rt, rs, rs_in, rq, rq_in, ex_in, ez, ez_in,
     load_sem, send_sem, recv_sem,
 ):
@@ -71,6 +71,8 @@
     y_peer = {d: freq_at(zh, step(y, d, Y), c) for d in (2, 1, 3)}
     steps = [(d, e) for d in (2, 1, 3, 0) for e in (2, 1, 3, 0) if d or e]
     xz_peer = {(d, e): frame_at(zq, step(zr, e, ZR), step(x, d, X)) for d, e in steps}
+    cells = [(d, e) for d in (2, 1, 3, 0) for e in (0, 1) if d or e]
+    cell_peer = {(d, e): freq_at(zh, step(y, d, Y), 1 - c if e else c) for d, e in cells}
     peers = [zh_peer, zq_peer, *xz_peer.values(), *y_peer.values(), core_peer]
 
     barrier = pltpu.get_barrier_semaphore()
@@ -164,7 +166,7 @@
         s = jnp.concatenate([spec[c_, i] for i in xs], axis=0)
         return inner(halves(s / outer(w, g)), g)
 
-    half, tail = Y * grows, pl.ds(grows, 8)
+    half = Y * grows
 
     for it in range(ITERS):
         order = (0, 1) if it else (zh, 1 - zh)
@@ -177,32 +179,33 @@
             fcore[it, c_, order[k], rows] = fcore[it, c_, order[k], rows] + terms if it else terms
 
         def send_core(k):
-            rows = pl.ds(0, half if k else half + 8)
-            return send(fcore.at[it, 1 - c, order[k], rows], fcore_in.at[it, order[k], rows], core_peer)
+            return send(fcore.at[it, 1 - c, order[k]], fcore_in.at[it, order[k]], core_peer)
+
+        def send_totals():
+            st[it] = fold8(wp[it])
+            return st[it], {
+                at: send(st.at[it], st_in.at[it, at[0], at[1]], cell_peer[at]) for at in cells
+            }
 
         def send_y(k, core):
-            h, n = order[k], grows if k else grows + 8
+            h = order[k]
             core.wait_recv()
             for i in range(Y):
                 rows = pl.ds(i * grows, grows)
-                fy[it, h, i, pl.ds(0, grows)] = fcore[it, c, h, rows] + fcore_in[it, h, rows]
-                if k == 0:
-                    rows = pl.ds(half, 8)
-                    fy[it, h, i, tail] = fcore[it, c, h, rows] + fcore_in[it, h, rows]
-            rows = pl.ds(0, n)
+                fy[it, h, i] = fcore[it, c, h, rows] + fcore_in[it, h, rows]
             return {
-                d: send(fy.at[it, h, step(y, d, Y), rows], fy_in.at[it, h, d - 1, rows], y_peer[d])
+                d: send(fy.at[it, h, step(y, d, Y)], fy_in.at[it, h, d - 1], y_peer[d])
                 for d in (2, 1, 3)
             }
 
         def send_far(k, near):
-            h, rows = order[k], pl.ds(0, grows if k else grows + 8)
-            total = fy[it, h, y, rows]
+            h = order[k]
+            total = fy[it, h, y]
             for d in (1, 3, 2):
                 near[d].wait_recv()
-                total = total + fy_in[it, h, d - 1, rows]
-            fz[it, h, rows] = total
-            return send(fz.at[it, h, rows], fz_in.at[it, h, rows], zh_peer)
+                total = total + fy_in[it, h, d - 1]
+            fz[it, h] = total
+            return send(fz.at[it, h], fz_in.at[it, h], zh_peer)
 
         if it:
             wait_all(part[0, e] for part in plane_parts for e in range(1, ZR))
@@ -211,19 +214,18 @@
                 for i in range(ZH):
                     fcore[it, c_, i, pl.ds(0, half)] = terms[i * half:(i + 1) * half]
             wait_all(part[at] for part in plane_parts for at in steps if at[0])
-        sums = fold8(wp[it])
-        for c_ in range(C):
-            fcore[it, c_, order[0], pl.ds(half, 8)] = sums
         xs = others if it else [x, *others]
         add_terms(1 - c, 0, xs)
         core = [send_core(0)]
         if it:
             add_terms(1 - c, 1, xs)
             core.append(send_core(1))
+            sums, totals = send_totals()
             add_terms(c, 0, xs)
             near = [send_y(0, core[0])]
             add_terms(c, 1, xs)
         else:
+            sums, totals = send_totals()
             add_terms(c, 0, xs)
             wait_all(cross)
             add_terms(1 - c, 1, xs)
@@ -231,6 +233,11 @@
             near = [send_y(0, core[0])]
             add_terms(c, 1, xs)
         near.append(send_y(1, core[1]))
+        for at in cells:
+            totals[at].wait_recv()
+            sums = sums + st_in[it, at[0], at[1]]
+        su[it] = sums
+        swap = send(su.at[it], su_in.at[it], zh_peer)
         far = [send_far(k, near[k]) for k in range(ZH)]
         drain(ZH)
         if it == 0:
@@ -242,9 +249,9 @@
             far[k].wait_recv()
             h = arrival[k]
             if k == 0:
-                scale = jnp.sum(fz[it, order[0], tail] + fz_in[it, h, tail], axis=0)
-            rows = pl.ds(0, grows)
-            gp[it + 1, c, h, y] = gp[it, c, h, y] * (fz[it, h, rows] + fz_in[it, h, rows]) / scale
+                swap.wait_recv()
+                scale = jnp.sum(su[it] + su_in[it], axis=0)
+            gp[it + 1, c, h, y] = gp[it, c, h, y] * (fz[it, h] + fz_in[it, h]) / scale
             mine = gp.at[it + 1, c, h, y]
             near.append(send_near(mine))
             cross.append(send(mine, mine, core_peer))
@@ -358,12 +365,16 @@
             pltpu.VMEM((X, C, frames // C, bins // X), F32),
             pltpu.VMEM((ITERS + 1, X, ZQ, ZR, wrows, K), F32),
             pltpu.VMEM((ITERS + 1, C, ZH, Y, grows, K), F32),
-            pltpu.VMEM((ITERS, C, ZH, Y * grows + 8, K), F32),
-            pltpu.VMEM((ITERS, ZH, Y * grows + 8, K), F32),
-            pltpu.VMEM((ITERS, ZH, Y, grows + 8, K), F32),
-            pltpu.VMEM((ITERS, ZH, Y - 1, grows + 8, K), F32),
-            pltpu.VMEM((ITERS, ZH, grows + 8, K), F32),
-            pltpu.VMEM((ITERS, ZH, grows + 8, K), F32),
+            pltpu.VMEM((ITERS, 8, K), F32),
+            pltpu.VMEM((ITERS, Y, C, 8, K), F32),
+            pltpu.VMEM((ITERS, 8, K), F32),
+            pltpu.VMEM((ITERS, 8, K), F32),
+            pltpu.VMEM((ITERS, C, ZH, Y * grows, K), F32),
+            pltpu.VMEM((ITERS, ZH, Y * grows, K), F32),
+            pltpu.VMEM((ITERS, ZH, Y, grows, K), F32),
+            pltpu.VMEM((ITERS, ZH, Y - 1, grows, K), F32),
+            pltpu.VMEM((ITERS, ZH, grows, K), F32),
+            pltpu.VMEM((ITERS, ZH, grows, K), F32),
             pltpu.VMEM((X, bins // X, K), F32),
             pltpu.VMEM((ITERS, X, ZQ, ZR, wrows, K), F32),
             pltpu.VMEM((X, ZQ, ZR, wrows, K), F32),

time: 100 us -> 101 us (1.010)
  no operation moved by 1% of the time
where the time goes in v9:
time: 101 us; the launch traced here: 100 us
  Pallas kernels  99.5 us (99%)
    pallas_call x1, Pallas kernels, per_device(): pl.pallas_call(kernel, out_shape=(pltpu.VMEM(basis.shape, F32), pltpu.VME...  98.9 us

profile of v9, /device:TPU:6, one launch (start us, length us, event | category | flops | bytes accessed | tf_op | source)
XLA Modules:
  0.0 100.2 jit_solution(11135732388837220777)
XLA Ops:
  0.6 98.9 %shard_map.50 = (f32[16,128]{1,0:T(8,128)S(1)}, f32[32,128]{1,0:T(8,128)S(1)}) custom-call(f32[8,4,16,512]{3,2,1,0:T(8,128)} %bitcast.1, f32[16,128]{1,0:T(8,128)} %basis_hbm.1, f32[32,128]{1,0:T(8,128)} %acts_hbm.1), custom_call_target="tpu_custom_call" | custom-call | tf_op jit(solution)/shard_map/pallas_call | solution.py:354
  99.5 0.6 shard_map.51

commit v10 on v7

--- a/solution.py
+++ b/solution.py
@@ -11,7 +11,7 @@
 Y, ZH, C = 4, 2, 2
 SEMS = 224
 GROUP = 2
-PAIRS = ((2, 1), (3, 0))
+PAIRS = ((2, 1, 3), (0,))
 F32, BF16 = jnp.float32, jnp.bfloat16
 
 

time: 100 us -> 101 us (1.010); the launches traced: 100 us -> 99.4 us
  no operation moved by 1% of the time
where the time goes in v10:
time: 101 us; the launch traced here: 99.4 us
  Pallas kernels  98.7 us (98%)
    pallas_call x1, Pallas kernels, per_device(): pl.pallas_call(kernel, out_shape=(pltpu.VMEM(basis.shape, F32), pltpu.VME...  98.1 us

profile of v10, /device:TPU:6, one launch (start us, length us, event | category | flops | bytes accessed | tf_op | source)
XLA Modules:
  0.0 99.4 jit_solution(8583330978120525801)
XLA Ops:
  0.6 98.1 %shard_map.50 = (f32[16,128]{1,0:T(8,128)S(1)}, f32[32,128]{1,0:T(8,128)S(1)}) custom-call(f32[8,4,16,512]{3,2,1,0:T(8,128)} %bitcast.1, f32[16,128]{1,0:T(8,128)} %basis_hbm.1, f32[32,128]{1,0:T(8,128)} %acts_hbm.1), custom_call_target="tpu_custom_call" | custom-call | tf_op jit(solution)/shard_map/pallas_call | solution.py:347
  98.7 0.6 shard_map.51
